TPU v7x, 768 devices: a whole 4x8x12 slice. The times are simulated.
768 devices in a mesh: dp: 64 (over z_hi, y, core), neg: 12 (over z_lo, x).
Axes of the slice: x: 4, y: 8, z: 12 (z_hi: 4, z_lo: 3; z = z_hi * 3 + z_lo), core: 2. Of those that a mesh axis runs over, the one named last changes fastest.
Arguments:
- img_features: bfloat16 [1536, 256, 1024], P(('dp', 'neg'))
- txt_features: bfloat16 [1536, 64, 1024], P(('dp', 'neg'))
- w_img: bfloat16 [1024, 256], replicated
- w_txt: bfloat16 [1024, 256], replicated
- cap_len: int32 [1536], P(('dp', 'neg')), may hold values from 16 to 64
- pairs: int32 [64, 24], P('dp'), may hold values from 0 to 23, each once within a row
Outputs:
- grad_img_features: bfloat16 [1536, 256, 1024], P(('dp', 'neg'))
- grad_txt_features: bfloat16 [1536, 64, 1024], P(('dp', 'neg'))
- grad_w_img: float32 [1024, 256], P('dp')
- grad_w_txt: float32 [1024, 256], P('dp')
Inputs may be any that keep to these rules, and one draw needn't show every extreme that they name: `pairs`: each row is a permutation of 0 to 23.
All inputs are finite; a program needn't handle non-finite values.
Results may differ from a plain program's by a relative error of at most 0.011.
Values may be sent and summed in bfloat16 or wider, within the bound.
No kernel may reach another device: no remote copies, remote signals or barrier semaphores. Data moves between devices by JAX's collectives and lax.ppermute only.
A program may use at most 64 MiB of HBM per device.

v0:
```python
import jax
import jax.numpy as jnp
from jax import lax
from jax.sharding import Mesh
from jax.sharding import PartitionSpec as P

NEG = ("neg_0", "neg_1")
DP_NEG = ("dp", "neg_0", "neg_1")


TOKEN_SCALE = 100.0
PAIR_SCALE = 50.0
EPSILON = 1e-06


def laid_out(pieces, dim):
    shape = list(pieces.shape[1:])
    shape[dim] *= pieces.shape[0]
    return jnp.moveaxis(pieces, 0, dim).reshape(shape)


def sent_to_all(array, axis):
    count = lax.axis_size(axis)
    return lax.all_to_all(
        jnp.broadcast_to(array[None], (count, *array.shape)), axis, 0, 0, tiled=True
    )


def gather_directly(array, axis, dim):
    return laid_out(sent_to_all(array, axis), dim)


def gathered_once(array, axis):
    leaves = jax.tree.leaves(array)
    sequence = sorted(range(len(leaves)), key=lambda k: -leaves[k].size)
    width = (1, *leaves[sequence[0]].shape)[-1]
    lines = [
        jnp.pad(leaves[k].reshape(-1), (0, -leaves[k].size % width)).reshape(-1, width)
        for k in sequence
    ]
    both, at, found = (lax.all_gather(jnp.concatenate(lines), axis), 0, {})
    for k, line in zip(sequence, lines):
        share = both[:, at : at + len(line)].reshape(len(both), -1)
        found[k] = share[:, : leaves[k].size].reshape(-1, *leaves[k].shape)
        at += len(line)
    numbers = iter(range(len(leaves)))
    return jax.tree.map(lambda _: found[next(numbers)], array)


def combined_by_axis(array, axes, combine):
    for axis in axes:
        pieces = gathered_once(array, axis)
        array = jax.tree.map(lambda part: part[0], pieces)
        for k in range(1, lax.axis_size(axis)):
            array = combine(array, jax.tree.map(lambda part: part[k], pieces))
    return array


def cut_along(array, dim, count):
    before, after = (array.shape[:dim], array.shape[dim + 1 :])
    return jnp.moveaxis(array.reshape(*before, count, -1, *after), dim, 0)


def sum_at_owner(array, axis, dim):
    pieces = cut_along(array, dim, lax.axis_size(axis))
    arrived = lax.all_to_all(pieces, axis, split_axis=0, concat_axis=0, tiled=True)
    return arrived.sum(axis=0)


def in_one_piece(arrays, axis, dim, along):
    both = jnp.concatenate(arrays, axis=along)
    filled, at, outs = (lax.psum_scatter(both, axis, scatter_dimension=dim, tiled=True), 0, [])
    for a in arrays:
        outs.append(lax.slice_in_dim(filled, at, at + a.shape[along], axis=along))
        at += a.shape[along]
    return tuple(outs)


def of_everyone(array, axis):
    everything = sent_to_all(array, axis)
    return jnp.sum(everything, axis=0)


def in_one(arrays, axis):
    line, at, outs = (jnp.concatenate([a.reshape(-1) for a in arrays]), 0, [])
    subtotal = of_everyone(line, axis)
    for a in arrays:
        outs.append(subtotal[at : at + a.size].reshape(a.shape))
        at += a.size
    return tuple(outs)


def unit_rows(projected):
    inverse = lax.rsqrt(jnp.sum(projected * projected, axis=-1, keepdims=True) + EPSILON)
    return (projected * inverse, inverse)


def back_unit(gradient, unit, inverse):
    return (gradient - unit * jnp.sum(unit * gradient, axis=-1, keepdims=True)) * inverse


def token_pool(scores, lengths, count_caps, text_len):
    rows = scores.shape[0]
    logits = (TOKEN_SCALE * scores).reshape(rows, count_caps, text_len)
    valid = (jnp.arange(text_len, dtype=jnp.int32)[None, :] < lengths[:, None])[None]
    peaks = jnp.max(jnp.where(valid, logits, -jnp.inf), axis=2, keepdims=True)
    expos = jnp.where(valid, jnp.exp(logits - peaks), 0.0)
    totals = jnp.sum(expos, axis=2, keepdims=True)
    pooled = (peaks[..., 0] + jnp.log(totals[..., 0])) / TOKEN_SCALE
    return (pooled, expos / totals)


def merge_stats(first, second):
    top = jnp.maximum(first[0], second[0])
    return (top, first[1] * jnp.exp(first[0] - top) + second[1] * jnp.exp(second[0] - top))


def shards(img_features, txt_features, w_img, w_txt, cap_len, pairs):
    local_count = img_features.shape[0]
    img_len = img_features.shape[1]
    text_len = txt_features.shape[1]
    width = w_img.shape[1]
    img_flat = img_features.reshape(local_count * img_len, img_features.shape[2])
    txt_flat = txt_features.reshape(local_count * text_len, txt_features.shape[2])
    img_unit, img_inv = unit_rows(jnp.dot(img_flat, w_img, preferred_element_type=jnp.float32))
    txt_unit, txt_inv = unit_rows(jnp.dot(txt_flat, w_txt, preferred_element_type=jnp.float32))
    img_half = img_unit.astype(jnp.bfloat16)
    txt_half = txt_unit.astype(jnp.bfloat16)
    group_text, group_len = (
        gather_directly(txt_half.reshape(local_count, text_len, width), NEG, 0),
        gather_directly(cap_len, NEG, 0),
    )
    group_size = group_text.shape[0]
    text_rows = group_text.reshape(group_size * text_len, width)
    scores = jnp.dot(img_half, text_rows.T, preferred_element_type=jnp.float32)
    pooled, weights = token_pool(scores, group_len, group_size, text_len)
    logits = PAIR_SCALE * jnp.mean(pooled.reshape(local_count, img_len, group_size), axis=1)
    row_prob = jax.nn.softmax(logits, axis=1)
    local_top = jnp.max(logits, axis=0)
    local_sum = jnp.sum(jnp.exp(logits - local_top[None, :]), axis=0)
    col_top, col_sum = combined_by_axis((local_top, local_sum), NEG, merge_stats)
    col_prob = jnp.exp(logits - col_top[None, :]) / col_sum[None, :]
    start = lax.axis_index(NEG) * local_count
    perm = lax.dynamic_slice_in_dim(pairs[0], start, local_count)
    target = (perm[:, None] == jnp.arange(group_size, dtype=jnp.int32)[None, :]).astype(jnp.float32)
    pair_grad = (row_prob + col_prob - 2.0 * target) * (PAIR_SCALE / (2.0 * group_size * img_len))
    spread = jnp.broadcast_to(pair_grad[:, None, :], (local_count, img_len, group_size))
    spread = spread.reshape(local_count * img_len, group_size, 1)
    score_grad = (
        (spread * weights)
        .reshape(local_count * img_len, group_size * text_len)
        .astype(jnp.bfloat16)
    )
    img_grad = jnp.dot(score_grad, text_rows, preferred_element_type=jnp.float32)
    text_terms = jnp.dot(score_grad.T, img_half, preferred_element_type=jnp.float32)
    txt_grad = sum_at_owner(text_terms.reshape(group_size, text_len, width), NEG, 0)
    txt_grad = txt_grad.reshape(local_count * text_len, width)
    img_back = back_unit(img_grad, img_unit, img_inv).astype(jnp.bfloat16)
    txt_back = back_unit(txt_grad, txt_unit, txt_inv).astype(jnp.bfloat16)
    feat_img = jnp.dot(img_back, w_img.T, preferred_element_type=jnp.float32).astype(jnp.bfloat16)
    feat_txt = jnp.dot(txt_back, w_txt.T, preferred_element_type=jnp.float32).astype(jnp.bfloat16)
    wgrad_img = jnp.dot(img_flat.T, img_back, preferred_element_type=jnp.float32)
    wgrad_txt = jnp.dot(txt_flat.T, txt_back, preferred_element_type=jnp.float32)
    share_img, share_txt = in_one_piece((wgrad_img, wgrad_txt), "dp", 0, 1)
    final_img, final_txt = in_one((share_img, share_txt), NEG)
    return (
        feat_img.reshape(img_features.shape),
        feat_txt.reshape(txt_features.shape),
        final_img,
        final_txt,
    )


def solution(mesh):
    split = Mesh(mesh.devices.reshape(mesh.shape["dp"], 3, 4), ("dp", "neg_0", "neg_1"))
    return jax.shard_map(
        shards,
        mesh=split,
        in_specs=(P(DP_NEG, None, None), P(DP_NEG, None, None), P(), P(), P(DP_NEG), P("dp", None)),
        out_specs=(P(DP_NEG, None, None), P(DP_NEG, None, None), P("dp", None), P("dp", None)),
        check_vma=False,
    )
```

profile of v0, /device:TPU:6, one launch (start us, length us, event | category | flops | bytes accessed | tf_op | source)
XLA Modules:
  0.0 324.6 jit_solution(5487772439366347421)
XLA Ops:
  8.6 12.8 %all-to-all-start = ((s32[12,1,2]{2,1,0:T(1,128)}), s32[12,1,2]{2,1,0:T(1,128)S(1)}, u32[]{:S(2)}, u32[]{:S(2)}) async-start(s32[12,1,2]{2,1,0:T(1,128)} %broadcast_in_dim.32), calls=%async_computation | async-start | bytes 12288 | tf_op jit(solution)/shard_map/all_to_all | solution.py:24
  22.9 3.5 %all-to-all-done = s32[12,1,2]{2,1,0:T(1,128)S(1)} async-done(((s32[12,1,2]{2,1,0:T(1,128)}), s32[12,1,2]{2,1,0:T(1,128)S(1)}, u32[]{:S(2)}, u32[]{:S(2)}) %all-to-all-start) | async-done | bytes 128 | tf_op jit(solution)/shard_map/all_to_all | solution.py:24
  27.3 5.6 %all-to-all-start.1 = ((bf16[12,2,64,256]{3,2,1,0:T(8,128)(2,1)}), bf16[12,2,64,256]{3,2,1,0:T(8,128)(2,1)S(1)}, u32[]{:S(2)}, u32[]{:S(2)}) async-start(bf16[12,2,64,256]{3,2,1,0:T(8,128)(2,1)} %broadcast_in_dim.35), calls=%async_computation.1 | async-start | bytes 1572864 | tf_op jit(solution)/shard_map/all_to_all | solution.py:24
  34.0 9.6 %all-to-all-done.1 = bf16[12,2,64,256]{3,2,1,0:T(8,128)(2,1)S(1)} async-done(((bf16[12,2,64,256]{3,2,1,0:T(8,128)(2,1)}), bf16[12,2,64,256]{3,2,1,0:T(8,128)(2,1)S(1)}, u32[]{:S(2)}, u32[]{:S(2)}) %all-to-all-start.1) | async-done | bytes 786464 | tf_op jit(solution)/shard_map/all_to_all | solution.py:24
  43.6 2.3 convolution_multiply_fusion
  45.9 3.6 %copy.28 = f32[512,1536]{0,1:T(8,128)} copy(f32[512,1536]{1,0:T(8,128)} %convolution_multiply_fusion) | data formatting | bytes 6291456 | tf_op jit(solution)/shard_map/mul | solution.py:104
  49.4 2.6 select_reduce_fusion.1
  53.7 5.1 %all-gather.2 = f32[3,2,24]{2,1,0:T(2,128)S(1)} all-gather(f32[1,2,24]{2,1,0:T(2,128)S(1)} %maximum_bitcast_fusion), channel_id=2, replica_groups=mesh['dp'=64,'neg_0'=3,'neg_1'=4] {'neg_0'}, dimensions={0}, use_global_device_ids=true | all-gather | bytes 768 | tf_op jit(solution)/shard_map/all_gather | solution.py:41
  58.9 6.9 %all-gather.3 = f32[4,2,24]{2,1,0:T(2,128)S(1)} all-gather(f32[1,2,24]{2,1,0:T(2,128)S(1)} %maximum_bitcast_fusion.1), channel_id=3, replica_groups=mesh['dp'=64,'neg_0'=3,'neg_1'=4] {'neg_1'}, dimensions={0}, use_global_device_ids=true | all-gather | bytes 960 | tf_op jit(solution)/shard_map/all_gather | solution.py:41
  66.0 2.1 mul.216
  68.1 3.6 %copy.31 = f32[512,1536]{1,0:T(8,128)} copy(f32[512,1536]{0,1:T(8,128)} %bitcast.193) | data formatting | bytes 6291456 | tf_op jit(solution)/shard_map/mul | solution.py:150
  71.7 2.0 div.52
  73.7 3.6 %copy.30 = f32[512,1536]{1,0:T(8,128)} copy(f32[512,1536]{0,1:T(8,128)} %bitcast.194) | data formatting | bytes 6291456 | tf_op jit(solution)/shard_map/div | solution.py:110
  77.3 2.1 sub.140
  79.4 3.5 %copy.29 = f32[512,1536]{1,0:T(8,128)} copy(f32[512,1536]{0,1:T(8,128)} %bitcast.195) | data formatting | bytes 6291456 | tf_op jit(solution)/shard_map/sub | solution.py:107
  82.9 6.0 %multiply_convert_fusion = bf16[512,1536]{1,0:T(8,128)(2,1)S(1)} fusion(f32[512,1536]{1,0:T(8,128)} %copy.31, f32[512,1536]{1,0:T(8,128)} %copy.30, f32[512,1536]{1,0:T(8,128)} %convolution_multiply_fusion, f32[512,1536]{1,0:T(8,128)} %copy.29, pred[1536]{0:T(1024)(128)(4,1)S(1)} %lt.42), kind=kLoop, calls=%fused_computation.1 | loop fusion | flops 3932160 | bytes 14157312 | tf_op jit(solution)/shard_map/convert_element_type | solution.py:152
  90.5 3.2 fusion
  93.7 7.5 %all-to-all-start.2 = ((f32[12,2,64,256]{3,2,1,0:T(8,128)}), f32[12,2,64,256]{3,2,1,0:T(8,128)}, u32[]{:S(2)}, u32[]{:S(2)}) async-start(f32[12,2,64,256]{3,2,1,0:T(8,128)} %fusion), calls=%async_computation.2 | async-start | bytes 3145728 | tf_op jit(solution)/shard_map/all_to_all | solution.py:66
  101.2 1.8 multiply_reduce_fusion
  104.5 13.3 %all-to-all-done.2 = f32[12,2,64,256]{3,2,1,0:T(8,128)} async-done(((f32[12,2,64,256]{3,2,1,0:T(8,128)}), f32[12,2,64,256]{3,2,1,0:T(8,128)}, u32[]{:S(2)}, u32[]{:S(2)}) %all-to-all-start.2) | async-done | bytes 1572896 | tf_op jit(solution)/shard_map/all_to_all | solution.py:66
  121.9 1.9 copy.38
  123.8 177.1 %reduce-scatter.4.cloned.1.call-done = f32[16,512]{1,0:T(8,128)} async-done(((f32[1024,512]{1,0:T(8,128)}), f32[16,512]{1,0:T(8,128)}) %reduce-scatter.4.cloned.1.call-update) | async-done | bytes 32784
  302.6 5.8 %all-to-all-start.3 = ((f32[12,1,8192]{2,1,0:T(1,128)}), f32[12,1,8192]{2,1,0:T(1,128)S(1)}, u32[]{:S(2)}, u32[]{:S(2)}) async-start(f32[12,1,8192]{2,1,0:T(1,128)} %broadcast_in_dim.71), calls=%async_computation.3 | async-start | bytes 786432 | tf_op jit(solution)/shard_map/all_to_all | solution.py:24
  310.9 5.3 %all-to-all-done.3 = f32[12,1,8192]{2,1,0:T(1,128)S(1)} async-done(((f32[12,1,8192]{2,1,0:T(1,128)}), f32[12,1,8192]{2,1,0:T(1,128)S(1)}, u32[]{:S(2)}, u32[]{:S(2)}) %all-to-all-start.3) | async-done | bytes 393248 | tf_op jit(solution)/shard_map/all_to_all | solution.py:24
  (71 shorter events, 19.8 us)
Async XLA Ops:
  7.2 25.9 %copy-start = (bf16[2,256,1024]{2,1,0:T(8,128)(2,1)S(1)}, bf16[2,256,1024]{2,1,0:T(8,128)(2,1)}, u32[]{:S(2)}) copy-start(bf16[2,256,1024]{2,1,0:T(8,128)(2,1)} %param.6) | copy-start | bytes 3145732
  7.2 25.8 %copy-start.9 = (s32[1,24]{1,0:T(1,128)S(1)}, s32[1,24]{1,0:T(1,128)}, u32[]{:S(2)}) copy-start(s32[1,24]{1,0:T(1,128)} %param.11) | copy-start | bytes 292
  7.2 25.9 %copy-start.3 = (bf16[1024,256]{1,0:T(8,128)(2,1)S(1)}, bf16[1024,256]{1,0:T(8,128)(2,1)}, u32[]{:S(2)}) copy-start(bf16[1024,256]{1,0:T(8,128)(2,1)} %param.8) | copy-start | bytes 1572868
  8.6 17.8 %all-to-all-start = ((s32[12,1,2]{2,1,0:T(1,128)}), s32[12,1,2]{2,1,0:T(1,128)S(1)}, u32[]{:S(2)}, u32[]{:S(2)}) async-start(s32[12,1,2]{2,1,0:T(1,128)} %broadcast_in_dim.32), calls=%async_computation | async-start | bytes 12288 | tf_op jit(solution)/shard_map/all_to_all | solution.py:24
  27.3 16.2 %all-to-all-start.1 = ((bf16[12,2,64,256]{3,2,1,0:T(8,128)(2,1)}), bf16[12,2,64,256]{3,2,1,0:T(8,128)(2,1)S(1)}, u32[]{:S(2)}, u32[]{:S(2)}) async-start(bf16[12,2,64,256]{3,2,1,0:T(8,128)(2,1)} %broadcast_in_dim.35), calls=%async_computation.1 | async-start | bytes 1572864 | tf_op jit(solution)/shard_map/all_to_all | solution.py:24
  43.6 5.9 %copy-start.2 = (bf16[12,2,64,256]{3,2,1,0:T(8,128)(2,1)}, bf16[12,2,64,256]{3,2,1,0:T(8,128)(2,1)S(1)}, u32[]{:S(2)}) copy-start(bf16[12,2,64,256]{3,2,1,0:T(8,128)(2,1)S(1)} %all-to-all-done.1) | copy-start | bytes 2359300
  49.4 2.8 copy-start.1
  93.7 24.1 %all-to-all-start.2 = ((f32[12,2,64,256]{3,2,1,0:T(8,128)}), f32[12,2,64,256]{3,2,1,0:T(8,128)}, u32[]{:S(2)}, u32[]{:S(2)}) async-start(f32[12,2,64,256]{3,2,1,0:T(8,128)} %fusion), calls=%async_computation.2 | async-start | bytes 3145728 | tf_op jit(solution)/shard_map/all_to_all | solution.py:66
  101.1 199.7 %reduce-scatter.4.cloned.1.call-start = ((), (), s32[]{:S(2)}) async-start(), calls=%async_computation.5 | async-start | bytes 2129920
  102.9 17.3 %copy-start.6 = (bf16[2,64,1024]{2,1,0:T(8,128)(2,1)S(1)}, bf16[2,64,1024]{2,1,0:T(8,128)(2,1)}, u32[]{:S(2)}) copy-start(bf16[2,64,1024]{2,1,0:T(8,128)(2,1)} %param.7) | copy-start | bytes 786436
  119.6 0.6 copy-start.7
  123.8 184.7 %copy-start.4 = (bf16[1024,256]{1,0:T(8,128)(2,1)S(1)}, bf16[1024,256]{1,0:T(8,128)(2,1)}, u32[]{:S(2)}) copy-start(bf16[1024,256]{1,0:T(8,128)(2,1)} %param.8) | copy-start | bytes 1572868
  123.8 186.2 %copy-start.5 = (bf16[1024,256]{1,0:T(8,128)(2,1)S(1)}, bf16[1024,256]{1,0:T(8,128)(2,1)}, u32[]{:S(2)}) copy-start(bf16[1024,256]{1,0:T(8,128)(2,1)} %param.9) | copy-start | bytes 1572868
  123.8 186.2 %copy-start.8 = (bf16[128,256]{1,0:T(8,128)(2,1)S(1)}, bf16[128,256]{1,0:T(8,128)(2,1)}, u32[]{:S(2)}) copy-start(bf16[128,256]{1,0:T(8,128)(2,1)} %copy-done.7) | copy-start | bytes 196612
  302.6 13.6 %all-to-all-start.3 = ((f32[12,1,8192]{2,1,0:T(1,128)}), f32[12,1,8192]{2,1,0:T(1,128)S(1)}, u32[]{:S(2)}, u32[]{:S(2)}) async-start(f32[12,1,8192]{2,1,0:T(1,128)} %broadcast_in_dim.71), calls=%async_computation.3 | async-start | bytes 786432 | tf_op jit(solution)/shard_map/all_to_all | solution.py:24
Sparse Core Ops, SparseCore 0:
  123.9 176.8 reduce-scatter.3
where the time goes:
time: 325 us
  waiting for transfers between devices  209 us (64%)
  starting transfers between devices  31.7 us (10%)
  local copies, waits for them, and re-layouts  30.7 us (9%)
  between operations  14.3 us (4%)
  other arithmetic  13.9 us (4%)
  matrix products  13.4 us (4%)
  blocking collectives  12.1 us (4%)
    unnamed x2, waiting for transfers between devices  177 us
    all_to_all x3, starting transfers between devices, sent_to_all(): lax.all_to_all(jnp.broadcast_to(array[None], (count, *array.shape)), axis...  24.2 us
    all_to_all x3, waiting for transfers between devices, sent_to_all(): lax.all_to_all(jnp.broadcast_to(array[None], (count, *array.shape)), axis...  18.4 us
    all_to_all x1, waiting for transfers between devices, sum_at_owner(): lax.all_to_all(pieces, axis, split_axis=0, concat_axis=0, tiled=True)  13.3 us
    all_gather x2, blocking collectives, gathered_once(): both, at, found = (lax.all_gather(jnp.concatenate(lines), axis), 0, {})  12.1 us
    all_to_all x1, starting transfers between devices, sum_at_owner(): lax.all_to_all(pieces, axis, split_axis=0, concat_axis=0, tiled=True)  7.5 us
  transfers between devices with their start and end apart: 5, of which 5 were waited for; matrix products, arithmetic and copies ran while one was open for 3% of the time, Pallas kernels for 0%

commit v1 on v0

v1 whole, which is shorter than its diff:
```python
import jax
import jax.numpy as jnp
from jax import lax
from jax.experimental import pallas as pl
from jax.experimental.pallas import tpu as pltpu
from jax.sharding import Mesh
from jax.sharding import PartitionSpec as P

NEG = ("neg_0", "neg_1")
DP_NEG = ("dp", "neg_0", "neg_1")

TOKEN_SCALE = 100.0
PAIR_SCALE = 50.0
EPSILON = 1e-06
LOG2E = 1.4426950408889634
LOW = -1e30
F32 = jnp.float32
BF16 = jnp.bfloat16

VMEM = pl.BlockSpec(memory_space=pltpu.VMEM)
SMEM = pl.BlockSpec(memory_space=pltpu.SMEM)


def call(kernel, outs, specs, flops, scratch=()):
    moved = sum(o.size * o.dtype.itemsize for o in outs)
    return pl.pallas_call(
        kernel,
        out_shape=tuple(outs),
        in_specs=specs,
        out_specs=tuple(VMEM for _ in outs),
        scratch_shapes=list(scratch),
        cost_estimate=pl.CostEstimate(flops=flops, bytes_accessed=2 * moved, transcendentals=0),
    )


def shape(dims, dtype):
    return jax.ShapeDtypeStruct(dims, dtype)


def along_rows(a, b):
    return lax.dot_general(a, b, (((0,), (0,)), ((), ())), preferred_element_type=F32)


def along_last(a, b):
    return lax.dot_general(a, b, (((1,), (1,)), ((), ())), preferred_element_type=F32)


def unit_rows(projected):
    inverse = lax.rsqrt(jnp.sum(projected * projected, axis=-1, keepdims=True) + EPSILON)
    return (projected * inverse, inverse)


def back_unit(gradient, unit, inverse):
    return (gradient - unit * jnp.sum(unit * gradient, axis=-1, keepdims=True)) * inverse


def text_kernel(len_ref, x_ref, w_ref, out_ref, unit_ref, inv_ref):
    unit, inverse = unit_rows(jnp.dot(x_ref[...], w_ref[...], preferred_element_type=F32))
    unit_ref[...] = unit
    inv_ref[...] = jnp.broadcast_to(inverse, inv_ref.shape)
    half = unit.astype(BF16)
    rows = half.shape[0]
    line = lax.broadcasted_iota(jnp.int32, (8, half.shape[1]), 0)
    lens = jnp.where(line == 0, len_ref[0], len_ref[1]).astype(F32).astype(BF16)
    for d in range(out_ref.shape[0]):
        out_ref[d, :rows, :] = half
        out_ref[d, rows:, :] = lens


def image_kernel(x_ref, w_ref, unit_ref, inv_ref, half_ref):
    unit, inverse = unit_rows(jnp.dot(x_ref[...], w_ref[...], preferred_element_type=F32))
    unit_ref[...] = unit
    inv_ref[...] = jnp.broadcast_to(inverse, inv_ref.shape)
    half_ref[...] = unit.astype(BF16)


def score_kernel(text_len, img_len, g_ref, half_ref, wt_ref, stats_ref, pooled_ref):
    owners = g_ref.shape[0]
    rows = 2 * text_len
    columns = half_ref.shape[0]
    half = half_ref[...]
    token = lax.broadcasted_iota(jnp.int32, (text_len, 128), 0).astype(F32)
    pooled_ref[...] = jnp.zeros_like(pooled_ref)
    for d in range(owners):
        scores = along_last(g_ref[d, :rows, :], half)
        lens = g_ref[d, rows:, :128].astype(F32)
        for j in range(2):
            keep = token < lens[j : j + 1, :]
            keep = jnp.concatenate([keep] * (columns // 128), axis=1)
            own = jnp.where(keep, scores[j * text_len : (j + 1) * text_len], LOW)
            top = jnp.max(own, axis=0, keepdims=True)
            expos = jnp.exp2((own - top) * (TOKEN_SCALE * LOG2E))
            total = jnp.sum(expos, axis=0, keepdims=True)
            b = 2 * d + j
            wt_ref[b * text_len : (b + 1) * text_len, :] = (expos * (1.0 / total)).astype(BF16)
            pooled_ref[b : b + 1, :] = top + jnp.log(total) / TOKEN_SCALE
    lane = lax.broadcasted_iota(jnp.int32, (128, 128), 1)
    first = jnp.sum(pooled_ref[:, :img_len], axis=1, keepdims=True)
    second = jnp.sum(pooled_ref[:, img_len:], axis=1, keepdims=True)
    table = jnp.where(lane == 0, first, second) * (PAIR_SCALE / img_len)
    logits = table.T[:8, :]
    line = lax.broadcasted_iota(jnp.int32, logits.shape, 0)
    logits = jnp.where(line < 2, logits, LOW)
    for d in range(owners):
        stats_ref[d] = logits


def terms_kernel(wt_ref, half_ref, terms_ref):
    img_len = half_ref.shape[0] // 2
    for a in range(2):
        part = slice(a * img_len, (a + 1) * img_len)
        terms_ref[a] = jnp.dot(wt_ref[:, part], half_ref[part, :], preferred_element_type=F32)


def pair_kernel(group_size, img_len, perm_ref, all_ref, own_ref, terms_ref, pay_ref, pair_ref):
    owners = all_ref.shape[0]
    text_len = pay_ref.shape[1] // 2
    everyone = all_ref[...].reshape(owners * 8, 128)
    col_top = jnp.max(everyone, axis=0, keepdims=True)
    col_sum = jnp.sum(jnp.exp(everyone - col_top), axis=0, keepdims=True)
    own = own_ref[0]
    lane = lax.broadcasted_iota(jnp.int32, own.shape, 1)
    line = lax.broadcasted_iota(jnp.int32, own.shape, 0)
    row = jnp.where(lane < group_size, own, LOW)
    expos = jnp.exp(row - jnp.max(row, axis=1, keepdims=True))
    row_prob = expos / jnp.sum(expos, axis=1, keepdims=True)
    col_prob = jnp.exp(own - col_top) / col_sum
    target = (lane == jnp.where(line == 0, perm_ref[0], perm_ref[1])).astype(F32)
    pair = (row_prob + col_prob - 2.0 * target) * (PAIR_SCALE / (2.0 * group_size * img_len))
    pair = jnp.concatenate([pair, jnp.zeros((120, 128), F32)], axis=0).T
    pair_ref[...] = pair
    for b in range(2 * owners):
        part = slice(b * text_len, (b + 1) * text_len)
        both = terms_ref[0, part, :] * pair[b : b + 1, 0:1] + terms_ref[1, part, :] * pair[b : b + 1, 1:2]
        pay_ref[b // 2, (b % 2) * text_len : (b % 2 + 1) * text_len, :] = both.astype(BF16)


def put_pieces(out_ref, grads):
    tiles = grads.reshape(-1, 16, grads.shape[1])
    for j in range(4):
        h, k = j // 2, j % 2
        piece = tiles[:, 8 * h : 8 * h + 8, 128 * k : 128 * k + 128]
        out_ref[j] = piece.reshape(out_ref.shape[1:]).astype(BF16)


def image_back_kernel(text_len, pair_ref, g_ref, wt_ref, unit_ref, inv_ref, x_ref, back_ref, pay_ref, scaled_ref):
    owners = g_ref.shape[0]
    img_len = unit_ref.shape[0] // 2
    for a in range(2):
        for b in range(2 * owners):
            text = g_ref[b // 2, (b % 2) * text_len : (b % 2 + 1) * text_len, :].astype(F32)
            scaled = text * pair_ref[b : b + 1, a : a + 1]
            scaled_ref[b * text_len : (b + 1) * text_len, :] = scaled.astype(BF16)
        part = slice(a * img_len, (a + 1) * img_len)
        gradient = along_rows(wt_ref[:, part], scaled_ref[...])
        back = back_unit(gradient, unit_ref[part, :], inv_ref[part, :1])
        back_ref[part, :] = back.astype(BF16)
    put_pieces(pay_ref, along_rows(x_ref[...], back_ref[...]))


def text_back_kernel(all_ref, unit_ref, inv_ref, x_ref, back_ref, pay_ref):
    gradient = all_ref[0].astype(F32)
    for d in range(1, all_ref.shape[0]):
        gradient += all_ref[d].astype(F32)
    back = back_unit(gradient, unit_ref[...], inv_ref[:, :1]).astype(BF16)
    back_ref[...] = back
    put_pieces(pay_ref, along_rows(x_ref[...], back))


def partial_kernel(all_ref, out_ref):
    total = all_ref[0].astype(F32)
    for d in range(1, all_ref.shape[0]):
        total += all_ref[d].astype(F32)
    out_ref[...] = total.astype(BF16).reshape(out_ref.shape)


def rows_kernel(img_ref, txt_ref, out_ref):
    img = jnp.sum(img_ref[...].astype(F32), axis=0)
    txt = jnp.sum(txt_ref[...].astype(F32), axis=0)
    for d in range(out_ref.shape[0]):
        out_ref[d, :8, :] = img
        out_ref[d, 8:, :] = txt


def final_kernel(outer, all_ref, img_ref, txt_ref):
    inner = all_ref.shape[0] // outer
    for j in range(inner):
        total = all_ref[j]
        for i in range(1, outer):
            total += all_ref[i * inner + j]
        h, k = j // 2, j % 2
        img_ref[8 * h : 8 * h + 8, 128 * k : 128 * k + 128] = total[:8]
        txt_ref[8 * h : 8 * h + 8, 128 * k : 128 * k + 128] = total[8:]


def swap(array, axis):
    return lax.all_to_all(array, axis, 0, 0, tiled=True)


def shards(img_features, txt_features, w_img, w_txt, cap_len, pairs):
    local_count, img_len, depth = img_features.shape
    text_len = txt_features.shape[1]
    width = w_img.shape[1]
    owners = lax.axis_size(NEG)
    outer = lax.axis_size("neg_0")
    dp = lax.axis_size("dp")
    group_size = owners * local_count
    img_rows, txt_rows = local_count * img_len, local_count * text_len
    img_flat = img_features.reshape(img_rows, depth)
    txt_flat = txt_features.reshape(txt_rows, depth)
    start = lax.axis_index(NEG) * local_count
    perm = lax.dynamic_slice_in_dim(pairs[0], start, local_count)

    sent, txt_unit, txt_inv = call(
        text_kernel,
        [shape((owners, txt_rows + 8, width), BF16), shape((txt_rows, width), F32), shape((txt_rows, 128), F32)],
        [SMEM, VMEM, VMEM],
        2 * txt_rows * depth * width,
    )(cap_len, txt_flat, w_txt)
    group = swap(sent, NEG)
    img_unit, img_inv, img_half = call(
        image_kernel,
        [shape((img_rows, width), F32), shape((img_rows, 128), F32), shape((img_rows, width), BF16)],
        [VMEM, VMEM],
        2 * img_rows * depth * width,
    )(img_flat, w_img)
    weights, own = call(
        lambda *refs: score_kernel(text_len, img_len, *refs),
        [shape((group_size * text_len, img_rows), BF16), shape((owners, 8, 128), F32)],
        [VMEM, VMEM],
        2 * group_size * text_len * img_rows * width,
        [pltpu.VMEM((128, img_rows), F32)],
    )(group, img_half)
    everyone = swap(own, NEG)
    (terms,) = call(
        terms_kernel,
        [shape((local_count, group_size * text_len, width), F32)],
        [VMEM, VMEM],
        2 * group_size * text_len * img_rows * width,
    )(weights, img_half)
    text_terms, pair = call(
        lambda *refs: pair_kernel(group_size, img_len, *refs),
        [shape((owners, txt_rows, width), BF16), shape((128, 128), F32)],
        [SMEM, VMEM, VMEM, VMEM],
        4 * group_size * text_len * width,
    )(perm, everyone, own, terms)
    arrived = swap(text_terms, NEG)
    img_back, img_pieces = call(
        lambda *refs: image_back_kernel(text_len, *refs),
        [shape((img_rows, width), BF16), shape((4, depth // 2, 128), BF16)],
        [VMEM] * 6,
        2 * img_rows * width * (group_size * text_len + depth),
        [pltpu.VMEM((group_size * text_len, width), BF16)],
    )(pair, group, weights, img_unit, img_inv, img_flat)
    img_quarter = swap(img_pieces, "neg_1")
    txt_back, txt_pieces = call(
        text_back_kernel,
        [shape((txt_rows, width), BF16), shape((4, depth // 2, 128), BF16)],
        [VMEM] * 4,
        2 * txt_rows * width * depth,
    )(arrived, txt_unit, txt_inv, txt_flat)
    txt_quarter = swap(txt_pieces, "neg_1")
    partial = lambda quarter: call(
        partial_kernel, [shape((dp, 8, 128), BF16)], [VMEM], 4 * depth * 64
    )(quarter)[0]
    img_rows_all = swap(partial(img_quarter), "dp")
    txt_rows_all = swap(partial(txt_quarter), "dp")
    (mine,) = call(
        rows_kernel, [shape((owners, 16, 128), F32)], [VMEM, VMEM], 2 * dp * 1024
    )(img_rows_all, txt_rows_all)
    final_img, final_txt = call(
        lambda *refs: final_kernel(outer, *refs),
        [shape((16, width), F32), shape((16, width), F32)],
        [VMEM],
        owners * 2048,
    )(swap(mine, NEG))
    feat_img = jnp.dot(img_back, w_img.T, preferred_element_type=F32).astype(BF16)
    feat_txt = jnp.dot(txt_back, w_txt.T, preferred_element_type=F32).astype(BF16)
    return (
        feat_img.reshape(img_features.shape),
        feat_txt.reshape(txt_features.shape),
        final_img,
        final_txt,
    )


def solution(mesh):
    split = Mesh(mesh.devices.reshape(mesh.shape["dp"], 3, 4), ("dp", "neg_0", "neg_1"))
    return jax.shard_map(
        shards,
        mesh=split,
        in_specs=(P(DP_NEG, None, None), P(DP_NEG, None, None), P(), P(), P(DP_NEG), P("dp", None)),
        out_specs=(P(DP_NEG, None, None), P(DP_NEG, None, None), P("dp", None), P("dp", None)),
        check_vma=False,
    )
```

time: 325 us -> 164 us (0.50)
  waiting for transfers between devices: 209 us -> 40.4 us
  starting transfers between devices: 31.7 us -> 64.3 us
  Pallas kernels: 0 us -> 30.1 us
  local copies, waits for them, and re-layouts: 30.7 us -> 2.77 us
  other arithmetic: 13.9 us -> 0 us
  between operations: 14.3 us -> 0.68 us
  matrix products: 13.4 us -> 2.46 us
  blocking collectives: 12.1 us -> 21 us
    unnamed x2 -> x0, waiting for transfers between devices: 177 us -> none
    all_to_all x4 -> x7, starting transfers between devices: 31.7 us -> 64.3 us  [swap(): return lax.all_to_all(array, axis, 0, 0, tiled=True)]
    pallas_call x0 -> x11, Pallas kernels: none -> 30.1 us  [the longest x1 4.4 us: shards(): call(lambda *refs: image_back_kernel(text_len, *refs), [shape((img_rows,...]
    all_to_all x0 -> x1, blocking collectives: none -> 21 us  [swap(): return lax.all_to_all(array, axis, 0, 0, tiled=True)]
    all_gather x2 -> x0, blocking collectives: 12.1 us -> none  [gathered_once(): both, at, found = (lax.all_gather(jnp.concatenate(lines), axis), 0, {})]
    dot_general x9 -> x2, matrix products: 13.4 us -> 2.46 us  [the longest x1 1.44 us: shards(): jnp.dot(img_back, w_img.T, preferred_element_type=F32).astype(BF16)]
    mul x3 -> x0, local copies, waits for them, and re-layouts: 9.26 us -> none  [the longest x2 5.68 us: shards(): spread * weights]
    all_to_all x4 -> x7, waiting for transfers between devices: 31.7 us -> 40.4 us  [swap(): return lax.all_to_all(array, axis, 0, 0, tiled=True)]
  transfers between devices with their start and end apart: 5 -> 7, of which waited for: 5 -> 7; matrix products, arithmetic and copies ran while one was open for 3% -> 2% of each run, Pallas kernels for 0% -> 11%
where the time goes in v1:
time: 164 us; the launch traced here: 162 us
  starting transfers between devices  64.3 us (39%)
  waiting for transfers between devices  40.4 us (25%)
  Pallas kernels  30.1 us (18%)
  blocking collectives  21 us (13%)
  local copies, waits for them, and re-layouts  2.77 us (2%)
  matrix products  2.46 us (2%)
    all_to_all x7, starting transfers between devices, swap(): return lax.all_to_all(array, axis, 0, 0, tiled=True)  64.3 us
    all_to_all x7, waiting for transfers between devices, swap(): return lax.all_to_all(array, axis, 0, 0, tiled=True)  40.4 us
    all_to_all x1, blocking collectives, swap(): return lax.all_to_all(array, axis, 0, 0, tiled=True)  21 us
    pallas_call x1, Pallas kernels, shards(): call(lambda *refs: image_back_kernel(text_len, *refs), [shape((img_rows,...  4.4 us
    pallas_call x1, Pallas kernels, shards(): call(lambda *refs: score_kernel(text_len, img_len, *refs), [shape((group_...  3.93 us
    pallas_call x1, Pallas kernels, shards(): call(terms_kernel, [shape((local_count, group_size * text_len, width), F3...  3.63 us
    pallas_call x2, Pallas kernels, shards(): call(partial_kernel, [shape((dp, 8, 128), BF16)], [VMEM], 4 * depth * 64)  3.59 us
    pallas_call x1, Pallas kernels, shards(): call(lambda *refs: pair_kernel(group_size, img_len, *refs), [shape((owner...  3.4 us
  transfers between devices with their start and end apart: 7, of which 7 were waited for; matrix products, arithmetic and copies ran while one was open for 2% of the time, Pallas kernels for 11%

profile of v1, /device:TPU:6, one launch (start us, length us, event | category | flops | bytes accessed | tf_op | source)
XLA Modules:
  0.0 161.8 jit_solution(2616621476280004361)
XLA Ops:
  0.6 2.4 %shard_map.93 = (bf16[12,136,256]{2,1,0:T(8,128)(2,1)}, f32[128,256]{1,0:T(8,128)}, f32[128,128]{1,0:T(8,128)}) custom-call(s32[2]{0:T(128)} %len_ref.1, bf16[128,1024]{1,0:T(8,128)(2,1)} %bitcast.13, bf16[1024,256]{1,0:T(8,128)(2,1)} %w_ref.2), custom_call_target="tpu_custom_call" | custom-call | flops 67108864 | bytes 2064384 | tf_op jit(solution)/shard_map/pallas_call | solution.py:214
  3.1 13.0 %all-to-all-start = ((bf16[12,136,256]{2,1,0:T(8,128)(2,1)}), bf16[12,136,256]{2,1,0:T(8,128)(2,1)S(1)}, u32[]{:S(2)}, u32[]{:S(2)}) async-start(bf16[12,136,256]{2,1,0:T(8,128)(2,1)} %get-tuple-element.20), calls=%async_computation | async-start | bytes 1671168 | tf_op jit(solution)/shard_map/all_to_all | solution.py:197
  16.1 2.9 %shard_map.94 = (f32[512,256]{1,0:T(8,128)}, f32[512,128]{1,0:T(8,128)}, bf16[512,256]{1,0:T(8,128)(2,1)}) custom-call(bf16[512,1024]{1,0:T(8,128)(2,1)} %bitcast.10, bf16[1024,256]{1,0:T(8,128)(2,1)} %w_ref.3), custom_call_target="tpu_custom_call" | custom-call | flops 268435456 | bytes 2097152 | tf_op jit(solution)/shard_map/pallas_call | solution.py:221
  19.0 8.2 %all-to-all-done.refs_0_.refs_1_ = bf16[12,136,256]{2,1,0:T(8,128)(2,1)S(1)} async-done(((bf16[12,136,256]{2,1,0:T(8,128)(2,1)}), bf16[12,136,256]{2,1,0:T(8,128)(2,1)S(1)}, u32[]{:S(2)}, u32[]{:S(2)}) %all-to-all-start) | async-done | bytes 835616 | tf_op jit(solution)/shard_map/all_to_all | solution.py:197
  28.0 3.9 %shard_map.95 = (bf16[1536,512]{1,0:T(8,128)(2,1)}, f32[12,8,128]{2,1,0:T(8,128)}) custom-call(bf16[12,136,256]{2,1,0:T(8,128)(2,1)} %copy-done.1, bf16[512,256]{1,0:T(8,128)(2,1)} %get-tuple-element.21.refs_1_.half_ref), custom_call_target="tpu_custom_call" | custom-call | flops 402653184 | bytes 3244032 | tf_op jit(solution)/shard_map/pallas_call | solution.py:227
  32.0 4.5 %all-to-all-start.1 = ((f32[12,8,128]{2,1,0:T(8,128)}), f32[12,8,128]{2,1,0:T(8,128)S(1)}, u32[]{:S(2)}, u32[]{:S(2)}) async-start(f32[12,8,128]{2,1,0:T(8,128)} %get-tuple-element.22.refs_2_), calls=%async_computation.1 | async-start | bytes 98304 | tf_op jit(solution)/shard_map/all_to_all | solution.py:197
  37.1 3.6 %shard_map.96.refs_3_ = f32[2,1536,256]{2,1,0:T(8,128)} custom-call(bf16[1536,512]{1,0:T(8,128)(2,1)} %get-tuple-element.23.wt_ref.refs_2_, bf16[512,256]{1,0:T(8,128)(2,1)} %get-tuple-element.21.refs_1_.half_ref), custom_call_target="tpu_custom_call" | custom-call | flops 402653184 | bytes 6291456 | tf_op jit(solution)/shard_map/pallas_call | solution.py:235
  42.4 3.4 %shard_map.97 = (bf16[12,128,256]{2,1,0:T(8,128)(2,1)}, f32[128,128]{1,0:T(8,128)}) custom-call(s32[2]{0:T(128)} %dynamic-slice_bitcast_fusion.refs_0_, f32[12,8,128]{2,1,0:T(8,128)} %copy-done.10, f32[12,8,128]{2,1,0:T(8,128)} %get-tuple-element.22.refs_2_, f32[2,1536,256]{2,1,0:T(8,128)} %shard_map.96.refs_3_), custom_call_target="tpu_custom_call" | custom-call | flops 1572864 | bytes 1703936 | tf_op jit(solution)/shard_map/pallas_call | solution.py:241
  45.8 5.5 %all-to-all-start.2 = ((bf16[12,128,256]{2,1,0:T(8,128)(2,1)}), bf16[12,128,256]{2,1,0:T(8,128)(2,1)S(1)}, u32[]{:S(2)}, u32[]{:S(2)}) async-start(bf16[12,128,256]{2,1,0:T(8,128)(2,1)} %get-tuple-element.28), calls=%async_computation.2 | async-start | bytes 1572864 | tf_op jit(solution)/shard_map/all_to_all | solution.py:197
  51.3 4.4 %shard_map.98 = (bf16[512,256]{1,0:T(8,128)(2,1)}, bf16[4,512,128]{2,1,0:T(8,128)(2,1)}) custom-call(f32[128,128]{1,0:T(8,128)} %get-tuple-element.24.refs_0_, bf16[12,136,256]{2,1,0:T(8,128)(2,1)} %copy-done.1, bf16[1536,512]{1,0:T(8,128)(2,1)} %get-tuple-element.23.wt_ref.refs_2_, f32[512,256]{1,0:T(8,128)} %get-tuple-element.25.refs_3_, ...), custom_call_target="tpu_custom_call" | custom-call | flops 671088640 | bytes 1572864 | tf_op jit(solution)/shard_map/pallas_call | solution.py:248
  55.7 6.3 %all-to-all-done.2.all_ref = bf16[12,128,256]{2,1,0:T(8,128)(2,1)S(1)} async-done(((bf16[12,128,256]{2,1,0:T(8,128)(2,1)}), bf16[12,128,256]{2,1,0:T(8,128)(2,1)S(1)}, u32[]{:S(2)}, u32[]{:S(2)}) %all-to-all-start.2) | async-done | bytes 786464 | tf_op jit(solution)/shard_map/all_to_all | solution.py:197
  62.0 4.5 %all-to-all-start.3 = ((bf16[4,512,128]{2,1,0:T(8,128)(2,1)}), bf16[4,512,128]{2,1,0:T(8,128)(2,1)S(1)}, u32[]{:S(2)}, u32[]{:S(2)}) async-start(bf16[4,512,128]{2,1,0:T(8,128)(2,1)} %get-tuple-element.32), calls=%async_computation.3 | async-start | bytes 1048576 | tf_op jit(solution)/shard_map/all_to_all | solution.py:197
  66.6 2.7 %shard_map.99 = (bf16[128,256]{1,0:T(8,128)(2,1)}, bf16[4,512,128]{2,1,0:T(8,128)(2,1)}) custom-call(bf16[12,128,256]{2,1,0:T(8,128)(2,1)} %copy-done.2, f32[128,256]{1,0:T(8,128)} %get-tuple-element.29.unit_ref, f32[128,128]{1,0:T(8,128)} %get-tuple-element.30.inv_ref, bf16[128,1024]{1,0:T(8,128)(2,1)} %bitcast.14), custom_call_target="tpu_custom_call" | custom-call | flops 67108864 | bytes 1179648 | tf_op jit(solution)/shard_map/pallas_call | solution.py:256
  69.2 4.3 %all-to-all-done.3.all_ref = bf16[4,512,128]{2,1,0:T(8,128)(2,1)S(1)} async-done(((bf16[4,512,128]{2,1,0:T(8,128)(2,1)}), bf16[4,512,128]{2,1,0:T(8,128)(2,1)S(1)}, u32[]{:S(2)}, u32[]{:S(2)}) %all-to-all-start.3) | async-done | bytes 524320 | tf_op jit(solution)/shard_map/all_to_all | solution.py:197
  73.5 5.5 %all-to-all-start.5 = ((bf16[4,512,128]{2,1,0:T(8,128)(2,1)}), bf16[4,512,128]{2,1,0:T(8,128)(2,1)S(1)}, u32[]{:S(2)}, u32[]{:S(2)}) async-start(bf16[4,512,128]{2,1,0:T(8,128)(2,1)} %get-tuple-element.33), calls=%async_computation.5 | async-start | bytes 1048576 | tf_op jit(solution)/shard_map/all_to_all | solution.py:197
  79.0 1.8 %shard_map.100 = bf16[64,8,128]{2,1,0:T(8,128)(2,1)} custom-call(bf16[4,512,128]{2,1,0:T(8,128)(2,1)} %copy-done.4), custom_call_target="tpu_custom_call" | custom-call | flops 262144 | bytes 262144 | tf_op jit(solution)/shard_map/pallas_call | solution.py:263
  80.9 4.2 %all-to-all-done.5.all_ref = bf16[4,512,128]{2,1,0:T(8,128)(2,1)S(1)} async-done(((bf16[4,512,128]{2,1,0:T(8,128)(2,1)}), bf16[4,512,128]{2,1,0:T(8,128)(2,1)S(1)}, u32[]{:S(2)}, u32[]{:S(2)}) %all-to-all-start.5) | async-done | bytes 524320 | tf_op jit(solution)/shard_map/all_to_all | solution.py:197
  85.0 25.9 %all-to-all-start.4 = ((bf16[64,8,128]{2,1,0:T(8,128)(2,1)}), bf16[64,8,128]{2,1,0:T(8,128)(2,1)S(1)}, u32[]{:S(2)}, u32[]{:S(2)}) async-start(bf16[64,8,128]{2,1,0:T(8,128)(2,1)} %shard_map.100), calls=%async_computation.4 | async-start | bytes 262144 | tf_op jit(solution)/shard_map/all_to_all | solution.py:197
  110.9 1.8 %shard_map.101 = bf16[64,8,128]{2,1,0:T(8,128)(2,1)} custom-call(bf16[4,512,128]{2,1,0:T(8,128)(2,1)} %copy-done.5), custom_call_target="tpu_custom_call" | custom-call | flops 262144 | bytes 262144 | tf_op jit(solution)/shard_map/pallas_call | solution.py:263
  112.7 13.1 %all-to-all-done.4.img_ref = bf16[64,8,128]{2,1,0:T(8,128)(2,1)S(1)} async-done(((bf16[64,8,128]{2,1,0:T(8,128)(2,1)}), bf16[64,8,128]{2,1,0:T(8,128)(2,1)S(1)}, u32[]{:S(2)}, u32[]{:S(2)}) %all-to-all-start.4) | async-done | bytes 131104 | tf_op jit(solution)/shard_map/all_to_all | solution.py:197
  125.8 21.0 %all_to_all.40.txt_ref = bf16[64,8,128]{2,1,0:T(8,128)(2,1)} all-to-all(bf16[64,8,128]{2,1,0:T(8,128)(2,1)} %shard_map.101), channel_id=1, replica_groups=mesh['dp'=64,'neg_0'=3,'neg_1'=4] {'dp'}, dimensions={0} | all-to-all | bytes 262144 | tf_op jit(solution)/shard_map/all_to_all | solution.py:197
  146.8 1.7 %shard_map.102 = f32[12,16,128]{2,1,0:T(8,128)} custom-call(bf16[64,8,128]{2,1,0:T(8,128)(2,1)} %copy-done.7, bf16[64,8,128]{2,1,0:T(8,128)(2,1)} %all_to_all.40.txt_ref), custom_call_target="tpu_custom_call" | custom-call | flops 131072 | bytes 196608 | tf_op jit(solution)/shard_map/pallas_call | solution.py:268
  148.5 5.4 %all-to-all-start.7 = ((f32[12,16,128]{2,1,0:T(8,128)}), f32[12,16,128]{2,1,0:T(8,128)S(1)}, u32[]{:S(2)}, u32[]{:S(2)}) async-start(f32[12,16,128]{2,1,0:T(8,128)} %shard_map.102), calls=%async_computation.7 | async-start | bytes 196608 | tf_op jit(solution)/shard_map/all_to_all | solution.py:197
  156.4 3.3 %all-to-all-done.7.refs_0_ = f32[12,16,128]{2,1,0:T(8,128)S(1)} async-done(((f32[12,16,128]{2,1,0:T(8,128)}), f32[12,16,128]{2,1,0:T(8,128)S(1)}, u32[]{:S(2)}, u32[]{:S(2)}) %all-to-all-start.7) | async-done | bytes 98336 | tf_op jit(solution)/shard_map/all_to_all | solution.py:197
  (29 shorter events, 7.9 us)
Async XLA Ops:
  0.6 35.8 %copy-start = (s32[1,24]{1,0:T(1,128)S(1)}, s32[1,24]{1,0:T(1,128)}, u32[]{:S(2)}) copy-start(s32[1,24]{1,0:T(1,128)} %param.11) | copy-start | bytes 292
  3.1 24.0 %all-to-all-start = ((bf16[12,136,256]{2,1,0:T(8,128)(2,1)}), bf16[12,136,256]{2,1,0:T(8,128)(2,1)S(1)}, u32[]{:S(2)}, u32[]{:S(2)}) async-start(bf16[12,136,256]{2,1,0:T(8,128)(2,1)} %get-tuple-element.20), calls=%async_computation | async-start | bytes 1671168 | tf_op jit(solution)/shard_map/all_to_all | solution.py:197
  27.1 0.9 copy-start.1
  32.0 9.9 %all-to-all-start.1 = ((f32[12,8,128]{2,1,0:T(8,128)}), f32[12,8,128]{2,1,0:T(8,128)S(1)}, u32[]{:S(2)}, u32[]{:S(2)}) async-start(f32[12,8,128]{2,1,0:T(8,128)} %get-tuple-element.22.refs_2_), calls=%async_computation.1 | async-start | bytes 98304 | tf_op jit(solution)/shard_map/all_to_all | solution.py:197
  41.8 0.6 copy-start.10
  45.8 16.2 %all-to-all-start.2 = ((bf16[12,128,256]{2,1,0:T(8,128)(2,1)}), bf16[12,128,256]{2,1,0:T(8,128)(2,1)S(1)}, u32[]{:S(2)}, u32[]{:S(2)}) async-start(bf16[12,128,256]{2,1,0:T(8,128)(2,1)} %get-tuple-element.28), calls=%async_computation.2 | async-start | bytes 1572864 | tf_op jit(solution)/shard_map/all_to_all | solution.py:197
  62.0 4.5 %copy-start.2 = (bf16[12,128,256]{2,1,0:T(8,128)(2,1)}, bf16[12,128,256]{2,1,0:T(8,128)(2,1)S(1)}, u32[]{:S(2)}) copy-start(bf16[12,128,256]{2,1,0:T(8,128)(2,1)S(1)} %all-to-all-done.2.all_ref) | copy-start | bytes 2359300
  62.0 11.5 %all-to-all-start.3 = ((bf16[4,512,128]{2,1,0:T(8,128)(2,1)}), bf16[4,512,128]{2,1,0:T(8,128)(2,1)S(1)}, u32[]{:S(2)}, u32[]{:S(2)}) async-start(bf16[4,512,128]{2,1,0:T(8,128)(2,1)} %get-tuple-element.32), calls=%async_computation.3 | async-start | bytes 1048576 | tf_op jit(solution)/shard_map/all_to_all | solution.py:197
  66.6 87.4 %copy-start.3 = (bf16[1024,256]{1,0:T(8,128)(2,1)S(1)}, bf16[1024,256]{1,0:T(8,128)(2,1)}, u32[]{:S(2)}) copy-start(bf16[1024,256]{1,0:T(8,128)(2,1)} %w_ref.3) | copy-start | bytes 1572868
  66.6 87.4 %copy-start.9 = (bf16[512,256]{1,0:T(8,128)(2,1)S(1)}, bf16[512,256]{1,0:T(8,128)(2,1)}, u32[]{:S(2)}) copy-start(bf16[512,256]{1,0:T(8,128)(2,1)} %get-tuple-element.27) | copy-start | bytes 786436
  73.5 5.5 %copy-start.4 = (bf16[4,512,128]{2,1,0:T(8,128)(2,1)}, bf16[4,512,128]{2,1,0:T(8,128)(2,1)S(1)}, u32[]{:S(2)}) copy-start(bf16[4,512,128]{2,1,0:T(8,128)(2,1)S(1)} %all-to-all-done.3.all_ref) | copy-start | bytes 1572868
  73.5 11.5 %all-to-all-start.5 = ((bf16[4,512,128]{2,1,0:T(8,128)(2,1)}), bf16[4,512,128]{2,1,0:T(8,128)(2,1)S(1)}, u32[]{:S(2)}, u32[]{:S(2)}) async-start(bf16[4,512,128]{2,1,0:T(8,128)(2,1)} %get-tuple-element.33), calls=%async_computation.5 | async-start | bytes 1048576 | tf_op jit(solution)/shard_map/all_to_all | solution.py:197
  79.0 76.3 %copy-start.6 = (bf16[1024,256]{1,0:T(8,128)(2,1)S(1)}, bf16[1024,256]{1,0:T(8,128)(2,1)}, u32[]{:S(2)}) copy-start(bf16[1024,256]{1,0:T(8,128)(2,1)} %w_ref.2) | copy-start | bytes 1572868
  79.0 76.3 %copy-start.11 = (bf16[128,256]{1,0:T(8,128)(2,1)S(1)}, bf16[128,256]{1,0:T(8,128)(2,1)}, u32[]{:S(2)}) copy-start(bf16[128,256]{1,0:T(8,128)(2,1)} %get-tuple-element.31) | copy-start | bytes 196612
  85.0 25.9 %copy-start.5 = (bf16[4,512,128]{2,1,0:T(8,128)(2,1)}, bf16[4,512,128]{2,1,0:T(8,128)(2,1)S(1)}, u32[]{:S(2)}) copy-start(bf16[4,512,128]{2,1,0:T(8,128)(2,1)S(1)} %all-to-all-done.5.all_ref) | copy-start | bytes 1572868
  85.0 40.7 %all-to-all-start.4 = ((bf16[64,8,128]{2,1,0:T(8,128)(2,1)}), bf16[64,8,128]{2,1,0:T(8,128)(2,1)S(1)}, u32[]{:S(2)}, u32[]{:S(2)}) async-start(bf16[64,8,128]{2,1,0:T(8,128)(2,1)} %shard_map.100), calls=%async_computation.4 | async-start | bytes 262144 | tf_op jit(solution)/shard_map/all_to_all | solution.py:197
  125.8 21.0 %copy-start.7 = (bf16[64,8,128]{2,1,0:T(8,128)(2,1)}, bf16[64,8,128]{2,1,0:T(8,128)(2,1)S(1)}, u32[]{:S(2)}) copy-start(bf16[64,8,128]{2,1,0:T(8,128)(2,1)S(1)} %all-to-all-done.4.img_ref) | copy-start | bytes 393220
  148.5 11.2 %all-to-all-start.7 = ((f32[12,16,128]{2,1,0:T(8,128)}), f32[12,16,128]{2,1,0:T(8,128)S(1)}, u32[]{:S(2)}, u32[]{:S(2)}) async-start(f32[12,16,128]{2,1,0:T(8,128)} %shard_map.102), calls=%async_computation.7 | async-start | bytes 196608 | tf_op jit(solution)/shard_map/all_to_all | solution.py:197
  159.7 0.6 copy-start.8

commit v2 on v1

v2 whole, which is shorter than its diff:
```python
import jax
import jax.numpy as jnp
from jax import lax
from jax.experimental import pallas as pl
from jax.experimental.pallas import tpu as pltpu
from jax.sharding import Mesh
from jax.sharding import PartitionSpec as P

NEG = ("neg_0", "neg_1")
DP_NEG = ("dp", "neg_0", "neg_1")

TOKEN_SCALE = 100.0
PAIR_SCALE = 50.0
EPSILON = 1e-06
LOG2E = 1.4426950408889634
LOW = -1e30
SCORE_GRANT = 52
PAIR_GRANT = 52
BACK_GRANT = 53
F32 = jnp.float32
BF16 = jnp.bfloat16

VMEM = pl.BlockSpec(memory_space=pltpu.VMEM)
SMEM = pl.BlockSpec(memory_space=pltpu.SMEM)
HBM = pl.BlockSpec(memory_space=pltpu.HBM)


def call(kernel, outs, specs, flops, scratch=(), grant=8, places=None):
    moved = sum(o.size * o.dtype.itemsize for o in outs)
    return pl.pallas_call(
        kernel,
        out_shape=tuple(outs),
        in_specs=specs,
        out_specs=tuple(places or [VMEM] * len(outs)),
        scratch_shapes=list(scratch),
        cost_estimate=pl.CostEstimate(flops=flops, bytes_accessed=2 * moved, transcendentals=0),
        compiler_params=pltpu.CompilerParams(vmem_limit_bytes=int(grant * 2**20)),
    )


def shape(dims, dtype):
    return jax.ShapeDtypeStruct(dims, dtype)


def along_rows(a, b):
    return lax.dot_general(a, b, (((0,), (0,)), ((), ())), preferred_element_type=F32)


def along_last(a, b):
    return lax.dot_general(a, b, (((1,), (1,)), ((), ())), preferred_element_type=F32)


def unit_rows(projected):
    inverse = lax.rsqrt(jnp.sum(projected * projected, axis=-1, keepdims=True) + EPSILON)
    return (projected * inverse, inverse)


def back_unit(gradient, unit, inverse):
    return (gradient - unit * jnp.sum(unit * gradient, axis=-1, keepdims=True)) * inverse


def copy(source, target, sem):
    moving = pltpu.make_async_copy(source, target, sem)
    moving.start()
    return moving


def text_kernel(len_ref, x_ref, w_ref, out_ref):
    unit, _ = unit_rows(jnp.dot(x_ref[...], w_ref[...], preferred_element_type=F32))
    half = unit.astype(BF16)
    rows, width = half.shape
    line = lax.broadcasted_iota(jnp.int32, (8, width), 0)
    lens = jnp.where(line == 0, len_ref[0], len_ref[1]).astype(F32).astype(BF16)
    for d in range(out_ref.shape[0]):
        out_ref[d, :rows, :] = half
        out_ref[d, rows:, :] = lens


def unit_kernel(x_ref, w_ref, unit_ref, inv_ref):
    unit, inverse = unit_rows(jnp.dot(x_ref[...], w_ref[...], preferred_element_type=F32))
    unit_ref[...] = unit
    inv_ref[...] = jnp.broadcast_to(inverse, inv_ref.shape)


def image_kernel(x_ref, w_ref, half_ref):
    unit, _ = unit_rows(jnp.dot(x_ref[...], w_ref[...], preferred_element_type=F32))
    half_ref[...] = unit.astype(BF16)


def score_kernel(text_len, img_len, g_ref, half_ref, wt_hbm, stats_hbm, wt_ref, pooled_ref, logits_ref, wt_sem, sem):
    owners = g_ref.shape[0]
    rows = 2 * text_len
    columns = half_ref.shape[0]
    half = half_ref[...]
    token = lax.broadcasted_iota(jnp.int32, (text_len, 128), 0).astype(F32)
    pooled_ref[...] = jnp.zeros_like(pooled_ref)
    moving = []
    for d in range(owners):
        scores = along_last(g_ref[d, :rows, :], half)
        lens = g_ref[d, rows:, :128].astype(F32)
        for j in range(2):
            keep = token < lens[j : j + 1, :]
            keep = jnp.concatenate([keep] * (columns // 128), axis=1)
            own = jnp.where(keep, scores[j * text_len : (j + 1) * text_len], LOW)
            top = jnp.max(own, axis=0, keepdims=True)
            expos = jnp.exp2((own - top) * (TOKEN_SCALE * LOG2E))
            total = jnp.sum(expos, axis=0, keepdims=True)
            b = 2 * d + j
            wt_ref[b * text_len : (b + 1) * text_len, :] = (expos * (1.0 / total)).astype(BF16)
            pooled_ref[b : b + 1, :] = top + jnp.log(total) / TOKEN_SCALE
        part = pl.ds(d * rows, rows)
        moving.append(copy(wt_ref.at[part, :], wt_hbm.at[part, :], wt_sem.at[d]))
    lane = lax.broadcasted_iota(jnp.int32, (128, 128), 1)
    first = jnp.sum(pooled_ref[:, :img_len], axis=1, keepdims=True)
    second = jnp.sum(pooled_ref[:, img_len:], axis=1, keepdims=True)
    table = jnp.where(lane == 0, first, second) * (PAIR_SCALE / img_len)
    logits = table.T[:8, :]
    line = lax.broadcasted_iota(jnp.int32, logits.shape, 0)
    logits_ref[...] = jnp.where(line < 2, logits, LOW)
    moving += [copy(logits_ref, stats_hbm.at[d], sem.at[d]) for d in range(owners)]
    for one in moving:
        one.wait()


def pair_kernel(
    group_size, img_len, pairs_ref, all_ref, own_ref, half_ref, wt_hbm, pay_hbm, pair_hbm,
    wt_ref, terms_ref, pair_ref, pay_ref, wt_sem, pair_sem, sem,
):
    owners = all_ref.shape[0]
    text_len = pay_ref.shape[1] // 2
    weights = copy(wt_hbm, wt_ref, wt_sem)
    start = (lax.axis_index("neg_0") * lax.axis_size("neg_1") + lax.axis_index("neg_1")) * 2
    everyone = all_ref[...].reshape(owners * 8, 128)
    col_top = jnp.max(everyone, axis=0, keepdims=True)
    col_sum = jnp.sum(jnp.exp(everyone - col_top), axis=0, keepdims=True)
    own = own_ref[0]
    lane = lax.broadcasted_iota(jnp.int32, own.shape, 1)
    line = lax.broadcasted_iota(jnp.int32, own.shape, 0)
    row = jnp.where(lane < group_size, own, LOW)
    expos = jnp.exp(row - jnp.max(row, axis=1, keepdims=True))
    row_prob = expos / jnp.sum(expos, axis=1, keepdims=True)
    col_prob = jnp.exp(own - col_top) / col_sum
    target = (lane == jnp.where(line == 0, pairs_ref[0, start], pairs_ref[0, start + 1])).astype(F32)
    pair = (row_prob + col_prob - 2.0 * target) * (PAIR_SCALE / (2.0 * group_size * img_len))
    pair = jnp.concatenate([pair, jnp.zeros((120, 128), F32)], axis=0).T
    pair_ref[...] = pair
    moving = [copy(pair_ref, pair_hbm.at[0], pair_sem)]
    weights.wait()
    for a in range(2):
        part = slice(a * img_len, (a + 1) * img_len)
        terms_ref[a] = jnp.dot(wt_ref[:, part], half_ref[part, :], preferred_element_type=F32)
    for d in range(owners):
        for j in range(2):
            b = 2 * d + j
            part = slice(b * text_len, (b + 1) * text_len)
            both = terms_ref[0, part, :] * pair[b : b + 1, 0:1] + terms_ref[1, part, :] * pair[b : b + 1, 1:2]
            pay_ref[d, j * text_len : (j + 1) * text_len, :] = both.astype(BF16)
        moving.append(copy(pay_ref.at[d], pay_hbm.at[d], sem.at[d]))
    for one in moving:
        one.wait()


def image_back_kernel(
    text_len, pair_hbm, g_hbm, wt_hbm, w_hbm, x_hbm, back_hbm, *refs
):
    turned, refs = refs[:4], refs[4:]
    pair_ref, g_ref, wt_ref, w_ref, x_ref, scaled_ref, back_ref, pay_ref, in_sem, out_sem = refs
    owners = g_ref.shape[0]
    pair = copy(pair_hbm.at[0], pair_ref, in_sem.at[4])
    group = copy(g_hbm, g_ref, in_sem.at[0])
    image = copy(x_hbm, x_ref, in_sem.at[1])
    projection = copy(w_hbm, w_ref, in_sem.at[2])
    weights = copy(wt_hbm, wt_ref, in_sem.at[3])
    img_len = x_ref.shape[0] // 2
    pair.wait()
    group.wait()
    for a in range(2):
        for b in range(2 * owners):
            text = g_ref[b // 2, (b % 2) * text_len : (b % 2 + 1) * text_len, :].astype(F32)
            scaled = text * pair_ref[b : b + 1, a : a + 1]
            scaled_ref[a, b * text_len : (b + 1) * text_len, :] = scaled.astype(BF16)
    image.wait()
    projection.wait()
    unit, inverse = unit_rows(jnp.dot(x_ref[...], w_ref[...], preferred_element_type=F32))
    weights.wait()
    for a in range(2):
        part = slice(a * img_len, (a + 1) * img_len)
        gradient = along_rows(wt_ref[:, part], scaled_ref[a])
        back_ref[part, :] = back_unit(gradient, unit[part], inverse[part]).astype(BF16)
    result = copy(back_ref, back_hbm, out_sem.at[4])
    tiles = along_rows(x_ref[...], back_ref[...]).reshape(-1, 16, back_ref.shape[1])
    for j in range(4):
        h, k = j // 2, j % 2
        piece = tiles[:, 8 * h : 8 * h + 8, 128 * k : 128 * k + 128]
        pay_ref[j] = piece.reshape(pay_ref.shape[1:]).astype(BF16)
    me = lax.axis_index("neg_1")
    moving = [
        copy(pay_ref.at[lax.rem(me + turn, 4)], target, out_sem.at[turn]) for turn, target in enumerate(turned)
    ]
    for one in moving:
        one.wait()
    result.wait()


def text_back_kernel(all_ref, unit_ref, inv_ref, x_ref, back_ref, pay_ref):
    gradient = all_ref[0].astype(F32)
    for d in range(1, all_ref.shape[0]):
        gradient += all_ref[d].astype(F32)
    back = back_unit(gradient, unit_ref[...], inv_ref[:, :1]).astype(BF16)
    back_ref[...] = back
    tiles = along_rows(x_ref[...], back).reshape(-1, 16, back.shape[1])
    for j in range(4):
        h, k = j // 2, j % 2
        piece = tiles[:, 8 * h : 8 * h + 8, 128 * k : 128 * k + 128]
        pay_ref[j] = piece.reshape(pay_ref.shape[1:]).astype(BF16)


def partial_kernel(*refs):
    images, txt_ref, out_ref = refs[:-2], refs[-2], refs[-1]
    groups = ([r[...] for r in images], [txt_ref[d] for d in range(txt_ref.shape[0])])
    for k, parts in enumerate(groups):
        total = parts[0].astype(F32)
        for part in parts[1:]:
            total += part.astype(F32)
        out_ref[:, 8 * k : 8 * k + 8, :] = total.astype(BF16).reshape(out_ref.shape[0], 8, 128)


def rows_kernel(all_ref, out_ref):
    total = jnp.sum(all_ref[...].astype(F32), axis=0)
    for d in range(out_ref.shape[0]):
        out_ref[d] = total


def final_kernel(outer, all_ref, img_ref, txt_ref):
    inner = all_ref.shape[0] // outer
    for j in range(inner):
        total = all_ref[j]
        for i in range(1, outer):
            total += all_ref[i * inner + j]
        h, k = j // 2, j % 2
        img_ref[8 * h : 8 * h + 8, 128 * k : 128 * k + 128] = total[:8]
        txt_ref[8 * h : 8 * h + 8, 128 * k : 128 * k + 128] = total[8:]


def swap(array, axis):
    return lax.all_to_all(array, axis, 0, 0, tiled=True)


def window(img_features, txt_features, w_img, w_txt, cap_len, pairs):
    local_count, img_len, depth = img_features.shape
    text_len = txt_features.shape[1]
    width = w_img.shape[1]
    owners = lax.axis_size(NEG)
    outer = lax.axis_size("neg_0")
    dp = lax.axis_size("dp")
    group_size = owners * local_count
    img_rows, txt_rows = local_count * img_len, local_count * text_len
    img_flat = img_features.reshape(img_rows, depth)
    txt_flat = txt_features.reshape(txt_rows, depth)
    DMA = pltpu.SemaphoreType.DMA

    (sent,) = call(
        text_kernel,
        [shape((owners, txt_rows + 8, width), BF16)],
        [SMEM, VMEM, VMEM],
        2 * txt_rows * depth * width,
        grant=63,
    )(cap_len, txt_flat, w_txt)
    group = swap(sent, NEG)
    (img_half,) = call(
        image_kernel, [shape((img_rows, width), BF16)], [VMEM, VMEM], 2 * img_rows * depth * width
    )(img_flat, w_img)
    weights, own = call(
        lambda *refs: score_kernel(text_len, img_len, *refs),
        [shape((group_size * text_len, img_rows), BF16), shape((owners, 8, 128), F32)],
        [VMEM, VMEM],
        2 * group_size * text_len * img_rows * width,
        [
            pltpu.VMEM((group_size * text_len, img_rows), BF16),
            pltpu.VMEM((128, img_rows), F32),
            pltpu.VMEM((8, 128), F32),
            DMA((owners,)),
            DMA((owners,)),
        ],
        places=[HBM, HBM],
        grant=SCORE_GRANT,
    )(group, img_half)
    everyone = swap(own, NEG)
    text_terms, pair = call(
        lambda *refs: pair_kernel(group_size, img_len, *refs),
        [shape((owners, txt_rows, width), BF16), shape((32, 128, 128), F32)],
        [SMEM, VMEM, VMEM, VMEM, HBM],
        2 * group_size * text_len * img_rows * width,
        [
            pltpu.VMEM((group_size * text_len, img_rows), BF16),
            pltpu.VMEM((local_count, group_size * text_len, width), F32),
            pltpu.VMEM((128, 128), F32),
            pltpu.VMEM((owners, txt_rows, width), BF16),
            DMA,
            DMA,
            DMA((owners,)),
        ],
        places=[HBM, HBM],
        grant=PAIR_GRANT,
    )(pairs, everyone, own, img_half, weights)
    arrived = swap(text_terms, NEG)
    img_back, *turned = call(
        lambda *refs: image_back_kernel(text_len, *refs),
        [shape((img_rows, width), BF16)] + [shape((depth // 2, 128), BF16)] * 4,
        [HBM, HBM, HBM, HBM, HBM],
        2 * img_rows * width * (group_size * text_len + depth),
        [
            pltpu.VMEM((128, 128), F32),
            pltpu.VMEM((owners, txt_rows + 8, width), BF16),
            pltpu.VMEM((group_size * text_len, img_rows), BF16),
            pltpu.VMEM((depth, width), BF16),
            pltpu.VMEM((img_rows, depth), BF16),
            pltpu.VMEM((2, group_size * text_len, width), BF16),
            pltpu.VMEM((img_rows, width), BF16),
            pltpu.VMEM((4, depth // 2, 128), BF16),
            DMA((5,)),
            DMA((5,)),
        ],
        places=[HBM] * 5,
        grant=BACK_GRANT,
    )(pair, group, weights, w_img, img_flat)
    for turn in range(1, 4):
        turned[turn] = lax.ppermute(turned[turn], "neg_1", [(k, (k + turn) % 4) for k in range(4)])
    txt_unit, txt_inv = call(
        unit_kernel,
        [shape((txt_rows, width), F32), shape((txt_rows, 128), F32)],
        [VMEM, VMEM],
        2 * txt_rows * width * depth,
    )(txt_flat, w_txt)
    txt_back, txt_pieces = call(
        text_back_kernel,
        [shape((txt_rows, width), BF16), shape((4, depth // 2, 128), BF16)],
        [VMEM] * 4,
        2 * txt_rows * width * depth,
    )(arrived, txt_unit, txt_inv, txt_flat)
    txt_quarter = swap(txt_pieces, "neg_1")
    (partial,) = call(partial_kernel, [shape((dp, 16, 128), BF16)], [VMEM] * 5, 8 * depth * 64)(
        *turned, txt_quarter
    )
    (mine,) = call(rows_kernel, [shape((owners, 16, 128), F32)], [VMEM], 2 * dp * 2048)(swap(partial, "dp"))
    final_img, final_txt = call(
        lambda *refs: final_kernel(outer, *refs),
        [shape((16, width), F32), shape((16, width), F32)],
        [VMEM],
        owners * 2048,
    )(swap(mine, NEG))
    feat_img = jnp.dot(img_back, w_img.T, preferred_element_type=F32).astype(BF16)
    feat_txt = jnp.dot(txt_back, w_txt.T, preferred_element_type=F32).astype(BF16)
    return (
        feat_img.reshape(img_features.shape),
        feat_txt.reshape(txt_features.shape),
        final_img,
        final_txt,
    )


def solution(mesh):
    split = Mesh(mesh.devices.reshape(mesh.shape["dp"], 3, 4), ("dp", "neg_0", "neg_1"))
    return jax.shard_map(
        window,
        mesh=split,
        in_specs=(P(DP_NEG, None, None), P(DP_NEG, None, None), P(), P(), P(DP_NEG), P("dp", None)),
        out_specs=(P(DP_NEG, None, None), P(DP_NEG, None, None), P("dp", None), P("dp", None)),
        check_vma=False,
    )
```

time: 164 us -> 143 us (0.87)
  blocking collectives: 21 us -> 52.2 us
  starting transfers between devices: 64.3 us -> 38.2 us
  Pallas kernels: 30.1 us -> 16.7 us
  waiting for transfers between devices: 40.4 us -> 30.3 us
  local copies, waits for them, and re-layouts: 2.77 us -> 0.92 us
    all_to_all x7 -> x4, starting transfers between devices: 64.3 us -> 29.4 us  [swap(): return lax.all_to_all(array, axis, 0, 0, tiled=True)]
    all_to_all x1 -> x2, blocking collectives: 21 us -> 52.2 us  [swap(): return lax.all_to_all(array, axis, 0, 0, tiled=True)]
    all_to_all x7 -> x4, waiting for transfers between devices: 40.4 us -> 24.2 us  [swap(): return lax.all_to_all(array, axis, 0, 0, tiled=True)]
    pallas_call x11 -> x10, Pallas kernels: 30.1 us -> 16.7 us  [the longest x1 4.86 us: window(): call(lambda *refs: image_back_kernel(text_len, *refs), [shape((img_rows,...]
    ppermute x0 -> x3, starting transfers between devices: none -> 8.79 us  [window(): lax.ppermute(turned[turn], 'neg_1', [(k, (k + turn) % 4) for k in range(4)])]
    ppermute x0 -> x3, waiting for transfers between devices: none -> 6.14 us  [window(): lax.ppermute(turned[turn], 'neg_1', [(k, (k + turn) % 4) for k in range(4)])]
  transfers between devices with their start and end apart: 7 -> 7, of which waited for: 7 -> 5; matrix products, arithmetic and copies ran while one was open for 2% -> 2% of each run, Pallas kernels for 11% -> 4%
where the time goes in v2:
time: 143 us; the launch traced here: 142 us
  blocking collectives  52.2 us (37%)
  starting transfers between devices  38.2 us (27%)
  waiting for transfers between devices  30.3 us (21%)
  Pallas kernels  16.7 us (12%)
  matrix products  2.45 us (2%)
    all_to_all x2, blocking collectives, swap(): return lax.all_to_all(array, axis, 0, 0, tiled=True)  52.2 us
    all_to_all x4, starting transfers between devices, swap(): return lax.all_to_all(array, axis, 0, 0, tiled=True)  29.4 us
    all_to_all x4, waiting for transfers between devices, swap(): return lax.all_to_all(array, axis, 0, 0, tiled=True)  24.2 us
    ppermute x3, starting transfers between devices, window(): lax.ppermute(turned[turn], 'neg_1', [(k, (k + turn) % 4) for k in range(4)])  8.79 us
    ppermute x3, waiting for transfers between devices, window(): lax.ppermute(turned[turn], 'neg_1', [(k, (k + turn) % 4) for k in range(4)])  6.14 us
    pallas_call x1, Pallas kernels, window(): call(lambda *refs: image_back_kernel(text_len, *refs), [shape((img_rows,...  4.86 us
    pallas_call x1, Pallas kernels, window(): call(lambda *refs: pair_kernel(group_size, img_len, *refs), [shape((owner...  3.36 us
  transfers between devices with their start and end apart: 7, of which 5 were waited for; matrix products, arithmetic and copies ran while one was open for 2% of the time, Pallas kernels for 4%

profile of v2, /device:TPU:6, one launch (start us, length us, event | category | flops | bytes accessed | tf_op | source)
XLA Modules:
  0.0 141.6 jit_solution(7450582037145139123)
XLA Ops:
  0.6 2.4 %shard_map.93 = bf16[12,136,256]{2,1,0:T(8,128)(2,1)} custom-call(s32[2]{0:T(128)} %len_ref.1, bf16[128,1024]{1,0:T(8,128)(2,1)} %bitcast.10, bf16[1024,256]{1,0:T(8,128)(2,1)} %w_ref.5), custom_call_target="tpu_custom_call" | custom-call | flops 67108864 | bytes 1671168 | tf_op jit(solution)/shard_map/pallas_call | solution.py:262
  3.1 13.1 %all-to-all-start = ((bf16[12,136,256]{2,1,0:T(8,128)(2,1)}), bf16[12,136,256]{2,1,0:T(8,128)(2,1)S(1)}, u32[]{:S(2)}, u32[]{:S(2)}) async-start(bf16[12,136,256]{2,1,0:T(8,128)(2,1)} %shard_map.93), calls=%async_computation | async-start | bytes 1671168 | tf_op jit(solution)/shard_map/all_to_all | solution.py:246
  16.8 10.5 %all-to-all-done.refs_0_.refs_1_ = bf16[12,136,256]{2,1,0:T(8,128)(2,1)S(1)} async-done(((bf16[12,136,256]{2,1,0:T(8,128)(2,1)}), bf16[12,136,256]{2,1,0:T(8,128)(2,1)S(1)}, u32[]{:S(2)}, u32[]{:S(2)}) %all-to-all-start) | async-done | bytes 835616 | tf_op jit(solution)/shard_map/all_to_all | solution.py:246
  27.2 2.4 %shard_map.95 = (bf16[1536,512]{1,0:T(8,128)(2,1)}, f32[12,8,128]{2,1,0:T(8,128)S(1)}) custom-call(bf16[12,136,256]{2,1,0:T(8,128)(2,1)S(1)} %all-to-all-done.refs_0_.refs_1_, bf16[512,256]{1,0:T(8,128)(2,1)S(1)} %shard_map.94.refs_1_.refs_3_), custom_call_target="tpu_custom_call" | custom-call | flops 402653184 | bytes 3244032 | tf_op jit(solution)/shard_map/pallas_call | solution.py:273
  29.7 0.9 copy-done.4
  30.6 9.8 %all_to_all.30.refs_1_ = f32[12,8,128]{2,1,0:T(8,128)S(1)} all-to-all(f32[12,8,128]{2,1,0:T(8,128)S(1)} %get-tuple-element.19.refs_2_), channel_id=1, replica_groups=mesh['dp'=64,'neg_0'=3,'neg_1'=4] {'neg_0','neg_1'}, dimensions={0} | all-to-all | bytes 98304 | tf_op jit(solution)/shard_map/all_to_all | solution.py:246
  40.3 3.4 %shard_map.96 = (bf16[12,128,256]{2,1,0:T(8,128)(2,1)}, f32[32,128,128]{2,1,0:T(8,128)}) custom-call(s32[1,24]{1,0:T(1,128)S(1)} %copy-done.6, f32[12,8,128]{2,1,0:T(8,128)S(1)} %all_to_all.30.refs_1_, f32[12,8,128]{2,1,0:T(8,128)S(1)} %get-tuple-element.19.refs_2_, bf16[512,256]{1,0:T(8,128)(2,1)S(1)} %shard_map.94.refs_1_.refs_3_, ...), custom_call_target="tpu_custom_call" | custom-call | flops 402653184 | bytes 5767168 | tf_op jit(solution)/shard_map/pallas_call | solution.py:289
  43.7 5.4 %all-to-all-start.2 = ((bf16[12,128,256]{2,1,0:T(8,128)(2,1)}), bf16[12,128,256]{2,1,0:T(8,128)(2,1)S(1)}, u32[]{:S(2)}, u32[]{:S(2)}) async-start(bf16[12,128,256]{2,1,0:T(8,128)(2,1)} %get-tuple-element.23), calls=%async_computation.2 | async-start | bytes 1572864 | tf_op jit(solution)/shard_map/all_to_all | solution.py:246
  49.5 10.4 %all-to-all-done.2.all_ref = bf16[12,128,256]{2,1,0:T(8,128)(2,1)S(1)} async-done(((bf16[12,128,256]{2,1,0:T(8,128)(2,1)}), bf16[12,128,256]{2,1,0:T(8,128)(2,1)S(1)}, u32[]{:S(2)}, u32[]{:S(2)}) %all-to-all-start.2) | async-done | bytes 786464 | tf_op jit(solution)/shard_map/all_to_all | solution.py:246
  59.9 1.3 shard_map.99
  61.2 4.5 %all-to-all-start.3 = ((bf16[4,512,128]{2,1,0:T(8,128)(2,1)}), bf16[4,512,128]{2,1,0:T(8,128)(2,1)S(1)}, u32[]{:S(2)}, u32[]{:S(2)}) async-start(bf16[4,512,128]{2,1,0:T(8,128)(2,1)} %get-tuple-element.31), calls=%async_computation.3 | async-start | bytes 1048576 | tf_op jit(solution)/shard_map/all_to_all | solution.py:246
  65.7 4.9 %shard_map.97 = (bf16[512,256]{1,0:T(8,128)(2,1)S(1)}, bf16[512,128]{1,0:T(8,128)(2,1)S(1)}, bf16[512,128]{1,0:T(8,128)(2,1)S(1)}, bf16[512,128]{1,0:T(8,128)(2,1)S(1)}, bf16[512,128]{1,0:T(8,128)(2,1)S(1)}) custom-call(f32[32,128,128]{2,1,0:T(8,128)} %get-tuple-element.21.refs_0_, bf16[12,136,256]{2,1,0:T(8,128)(2,1)} %copy-done.4, ...), custom_call_target="tpu_custom_call" | custom-call | flops 671088640 | bytes 1572864 | tf_op jit(solution)/shard_map/pallas_call | solution.py:307
  70.6 2.1 %collective-permute-start = (bf16[512,128]{1,0:T(8,128)(2,1)S(1)}, bf16[512,128]{1,0:T(8,128)(2,1)S(1)}, u32[]{:S(2)}, u32[]{:S(2)}) collective-permute-start(bf16[512,128]{1,0:T(8,128)(2,1)S(1)} %get-tuple-element.28), channel_id=1, source_target_pairs={{0,1},{1,2},{2,3},{3,0},{4,5},{5,6},{6,7},{7,4},{8,9},{9,10},{10,1... | collective-permute-start | bytes 393224 | tf_op jit(solution)/shard_map/ppermute | solution.py:328
  72.6 4.8 %collective-permute-start.1 = (bf16[512,128]{1,0:T(8,128)(2,1)S(1)}, bf16[512,128]{1,0:T(8,128)(2,1)S(1)}, u32[]{:S(2)}, u32[]{:S(2)}) collective-permute-start(bf16[512,128]{1,0:T(8,128)(2,1)S(1)} %get-tuple-element.29), channel_id=1, source_target_pairs={{0,2},{1,3},{2,0},{3,1},{4,6},{5,7},{6,4},{7,5},{8,10},{9,11},{10,... | collective-permute-start | bytes 393224 | tf_op jit(solution)/shard_map/ppermute | solution.py:328
  77.5 1.9 %collective-permute-start.2 = (bf16[512,128]{1,0:T(8,128)(2,1)S(1)}, bf16[512,128]{1,0:T(8,128)(2,1)S(1)}, u32[]{:S(2)}, u32[]{:S(2)}) collective-permute-start(bf16[512,128]{1,0:T(8,128)(2,1)S(1)} %get-tuple-element.30), channel_id=1, source_target_pairs={{0,3},{1,0},{2,1},{3,2},{4,7},{5,4},{6,5},{7,6},{8,11},{9,8},{10,9... | collective-permute-start | bytes 393224 | tf_op jit(solution)/shard_map/ppermute | solution.py:328
  79.4 1.6 %collective-permute-done.1.refs_2_ = bf16[512,128]{1,0:T(8,128)(2,1)S(1)} collective-permute-done((bf16[512,128]{1,0:T(8,128)(2,1)S(1)}, bf16[512,128]{1,0:T(8,128)(2,1)S(1)}, u32[]{:S(2)}, u32[]{:S(2)}) %collective-permute-start.1) | collective-permute-done | bytes 131104 | tf_op jit(solution)/shard_map/ppermute | solution.py:328
  81.0 4.5 %collective-permute-done.2.refs_3_ = bf16[512,128]{1,0:T(8,128)(2,1)S(1)} collective-permute-done((bf16[512,128]{1,0:T(8,128)(2,1)S(1)}, bf16[512,128]{1,0:T(8,128)(2,1)S(1)}, u32[]{:S(2)}, u32[]{:S(2)}) %collective-permute-start.2) | collective-permute-done | bytes 131104 | tf_op jit(solution)/shard_map/ppermute | solution.py:328
  85.7 42.5 %all_to_all.31.all_ref = bf16[64,16,128]{2,1,0:T(8,128)(2,1)S(1)} all-to-all(bf16[64,16,128]{2,1,0:T(8,128)(2,1)S(1)} %shard_map.100), channel_id=1, replica_groups=mesh['dp'=64,'neg_0'=3,'neg_1'=4] {'dp'}, dimensions={0} | all-to-all | bytes 524288 | tf_op jit(solution)/shard_map/all_to_all | solution.py:246
  128.1 0.7 shard_map.101
  128.8 6.4 %all-to-all-start.5 = ((f32[12,16,128]{2,1,0:T(8,128)}), f32[12,16,128]{2,1,0:T(8,128)S(1)}, u32[]{:S(2)}, u32[]{:S(2)}) async-start(f32[12,16,128]{2,1,0:T(8,128)} %shard_map.101), calls=%async_computation.5 | async-start | bytes 196608 | tf_op jit(solution)/shard_map/all_to_all | solution.py:246
  135.2 1.4 %convolution_convert_fusion = bf16[512,1024]{1,0:T(8,128)(2,1)} fusion(bf16[512,256]{1,0:T(8,128)(2,1)S(1)} %get-tuple-element.22, bf16[1024,256]{1,0:T(8,128)(2,1)S(1)} %copy-done.1), kind=kOutput, calls=%fused_computation | convolution fusion | flops 268959744 | bytes 1835008 | tf_op jit(solution)/shard_map/dot_general | solution.py:352
  136.7 1.0 convolution_convert_fusion.1
  137.7 3.3 %all-to-all-done.5.refs_0_ = f32[12,16,128]{2,1,0:T(8,128)S(1)} async-done(((f32[12,16,128]{2,1,0:T(8,128)}), f32[12,16,128]{2,1,0:T(8,128)S(1)}, u32[]{:S(2)}, u32[]{:S(2)}) %all-to-all-start.5) | async-done | bytes 98336 | tf_op jit(solution)/shard_map/all_to_all | solution.py:246
  140.9 0.6 shard_map.102
  (18 shorter events, 1.0 us)
Async XLA Ops:
  0.6 15.6 %copy-start = (bf16[1024,256]{1,0:T(8,128)(2,1)S(1)}, bf16[1024,256]{1,0:T(8,128)(2,1)}, u32[]{:S(2)}) copy-start(bf16[1024,256]{1,0:T(8,128)(2,1)} %refs_3_.1) | copy-start | bytes 1572868
  3.1 13.2 %copy-start.3 = (bf16[2,256,1024]{2,1,0:T(8,128)(2,1)S(1)}, bf16[2,256,1024]{2,1,0:T(8,128)(2,1)}, u32[]{:S(2)}) copy-start(bf16[2,256,1024]{2,1,0:T(8,128)(2,1)} %param.6) | copy-start | bytes 3145732
  3.1 24.2 %all-to-all-start = ((bf16[12,136,256]{2,1,0:T(8,128)(2,1)}), bf16[12,136,256]{2,1,0:T(8,128)(2,1)S(1)}, u32[]{:S(2)}, u32[]{:S(2)}) async-start(bf16[12,136,256]{2,1,0:T(8,128)(2,1)} %shard_map.93), calls=%async_computation | async-start | bytes 1671168 | tf_op jit(solution)/shard_map/all_to_all | solution.py:246
  16.2 24.1 %copy-start.6 = (s32[1,24]{1,0:T(1,128)S(1)}, s32[1,24]{1,0:T(1,128)}, u32[]{:S(2)}) copy-start(s32[1,24]{1,0:T(1,128)} %refs_0_.1) | copy-start | bytes 292
  29.7 0.9 copy-start.4
  30.6 18.6 %copy-start.2 = (bf16[1024,256]{1,0:T(8,128)(2,1)S(1)}, bf16[1024,256]{1,0:T(8,128)(2,1)}, u32[]{:S(2)}) copy-start(bf16[1024,256]{1,0:T(8,128)(2,1)} %w_ref.5) | copy-start | bytes 1572868
  30.6 18.6 %copy-start.5 = (bf16[2,64,1024]{2,1,0:T(8,128)(2,1)S(1)}, bf16[2,64,1024]{2,1,0:T(8,128)(2,1)}, u32[]{:S(2)}) copy-start(bf16[2,64,1024]{2,1,0:T(8,128)(2,1)} %param.7) | copy-start | bytes 786436
  43.7 16.2 %all-to-all-start.2 = ((bf16[12,128,256]{2,1,0:T(8,128)(2,1)}), bf16[12,128,256]{2,1,0:T(8,128)(2,1)S(1)}, u32[]{:S(2)}, u32[]{:S(2)}) async-start(bf16[12,128,256]{2,1,0:T(8,128)(2,1)} %get-tuple-element.23), calls=%async_computation.2 | async-start | bytes 1572864 | tf_op jit(solution)/shard_map/all_to_all | solution.py:246
  61.2 24.3 %all-to-all-start.3 = ((bf16[4,512,128]{2,1,0:T(8,128)(2,1)}), bf16[4,512,128]{2,1,0:T(8,128)(2,1)S(1)}, u32[]{:S(2)}, u32[]{:S(2)}) async-start(bf16[4,512,128]{2,1,0:T(8,128)(2,1)} %get-tuple-element.31), calls=%async_computation.3 | async-start | bytes 1048576 | tf_op jit(solution)/shard_map/all_to_all | solution.py:246
  70.6 64.7 %copy-start.1 = (bf16[1024,256]{1,0:T(8,128)(2,1)S(1)}, bf16[1024,256]{1,0:T(8,128)(2,1)}, u32[]{:S(2)}) copy-start(bf16[1024,256]{1,0:T(8,128)(2,1)} %refs_3_.1) | copy-start | bytes 1572868
  70.6 8.8 %collective-permute-start = (bf16[512,128]{1,0:T(8,128)(2,1)S(1)}, bf16[512,128]{1,0:T(8,128)(2,1)S(1)}, u32[]{:S(2)}, u32[]{:S(2)}) collective-permute-start(bf16[512,128]{1,0:T(8,128)(2,1)S(1)} %get-tuple-element.28), channel_id=1, source_target_pairs={{0,1},{1,2},{2,3},{3,0},{4,5},{5,6},{6,7},{7,4},{8,9},{9,10},{10,1... | collective-permute-start | bytes 393224 | tf_op jit(solution)/shard_map/ppermute | solution.py:328
  72.6 8.4 %collective-permute-start.1 = (bf16[512,128]{1,0:T(8,128)(2,1)S(1)}, bf16[512,128]{1,0:T(8,128)(2,1)S(1)}, u32[]{:S(2)}, u32[]{:S(2)}) collective-permute-start(bf16[512,128]{1,0:T(8,128)(2,1)S(1)} %get-tuple-element.29), channel_id=1, source_target_pairs={{0,2},{1,3},{2,0},{3,1},{4,6},{5,7},{6,4},{7,5},{8,10},{9,11},{10,... | collective-permute-start | bytes 393224 | tf_op jit(solution)/shard_map/ppermute | solution.py:328
  77.5 8.1 %collective-permute-start.2 = (bf16[512,128]{1,0:T(8,128)(2,1)S(1)}, bf16[512,128]{1,0:T(8,128)(2,1)S(1)}, u32[]{:S(2)}, u32[]{:S(2)}) collective-permute-start(bf16[512,128]{1,0:T(8,128)(2,1)S(1)} %get-tuple-element.30), channel_id=1, source_target_pairs={{0,3},{1,0},{2,1},{3,2},{4,7},{5,4},{6,5},{7,6},{8,11},{9,8},{10,9... | collective-permute-start | bytes 393224 | tf_op jit(solution)/shard_map/ppermute | solution.py:328
  128.8 12.1 %all-to-all-start.5 = ((f32[12,16,128]{2,1,0:T(8,128)}), f32[12,16,128]{2,1,0:T(8,128)S(1)}, u32[]{:S(2)}, u32[]{:S(2)}) async-start(f32[12,16,128]{2,1,0:T(8,128)} %shard_map.101), calls=%async_computation.5 | async-start | bytes 196608 | tf_op jit(solution)/shard_map/all_to_all | solution.py:246

commit v3 on v2

--- a/solution.py
+++ b/solution.py
@@ -17,6 +17,7 @@
 SCORE_GRANT = 52
 PAIR_GRANT = 52
 BACK_GRANT = 53
+FEATURE_GRANT = 53
 F32 = jnp.float32
 BF16 = jnp.bfloat16
 
@@ -124,11 +125,14 @@
 
 def pair_kernel(
     group_size, img_len, pairs_ref, all_ref, own_ref, half_ref, wt_hbm, pay_hbm, pair_hbm,
-    wt_ref, terms_ref, pair_ref, pay_ref, wt_sem, pair_sem, sem,
+    wt_ref, pair_ref, pay_ref, wt_sem, pair_sem, sem,
 ):
     owners = all_ref.shape[0]
     text_len = pay_ref.shape[1] // 2
-    weights = copy(wt_hbm, wt_ref, wt_sem)
+    rows = wt_hbm.shape[0] // 3
+    weights = [
+        copy(wt_hbm.at[pl.ds(k * rows, rows), :], wt_ref.at[pl.ds(k * rows, rows), :], wt_sem.at[k]) for k in range(3)
+    ]
     start = (lax.axis_index("neg_0") * lax.axis_size("neg_1") + lax.axis_index("neg_1")) * 2
     everyone = all_ref[...].reshape(owners * 8, 128)
     col_top = jnp.max(everyone, axis=0, keepdims=True)
@@ -145,17 +149,17 @@
     pair = jnp.concatenate([pair, jnp.zeros((120, 128), F32)], axis=0).T
     pair_ref[...] = pair
     moving = [copy(pair_ref, pair_hbm.at[0], pair_sem)]
-    weights.wait()
-    for a in range(2):
-        part = slice(a * img_len, (a + 1) * img_len)
-        terms_ref[a] = jnp.dot(wt_ref[:, part], half_ref[part, :], preferred_element_type=F32)
-    for d in range(owners):
-        for j in range(2):
-            b = 2 * d + j
-            part = slice(b * text_len, (b + 1) * text_len)
-            both = terms_ref[0, part, :] * pair[b : b + 1, 0:1] + terms_ref[1, part, :] * pair[b : b + 1, 1:2]
+    for k in range(3):
+        weights[k].wait()
+        first = jnp.dot(wt_ref[k * rows : (k + 1) * rows, :img_len], half_ref[:img_len, :], preferred_element_type=F32)
+        second = jnp.dot(wt_ref[k * rows : (k + 1) * rows, img_len:], half_ref[img_len:, :], preferred_element_type=F32)
+        for b in range(k * rows // text_len, (k + 1) * rows // text_len):
+            part = slice(b * text_len - k * rows, (b + 1) * text_len - k * rows)
+            both = first[part] * pair[b : b + 1, 0:1] + second[part] * pair[b : b + 1, 1:2]
+            d, j = b // 2, b % 2
             pay_ref[d, j * text_len : (j + 1) * text_len, :] = both.astype(BF16)
-        moving.append(copy(pay_ref.at[d], pay_hbm.at[d], sem.at[d]))
+            if j:
+                moving.append(copy(pay_ref.at[d], pay_hbm.at[d], sem.at[d]))
     for one in moving:
         one.wait()
 
@@ -215,6 +219,11 @@
         pay_ref[j] = piece.reshape(pay_ref.shape[1:]).astype(BF16)
 
 
+def feature_kernel(img_ref, w_img_ref, txt_ref, w_txt_ref, img_out, txt_out):
+    img_out[...] = along_last(img_ref[...], w_img_ref[...]).astype(BF16)
+    txt_out[...] = along_last(txt_ref[...], w_txt_ref[...]).astype(BF16)
+
+
 def partial_kernel(*refs):
     images, txt_ref, out_ref = refs[:-2], refs[-2], refs[-1]
     groups = ([r[...] for r in images], [txt_ref[d] for d in range(txt_ref.shape[0])])
@@ -293,10 +302,9 @@
         2 * group_size * text_len * img_rows * width,
         [
             pltpu.VMEM((group_size * text_len, img_rows), BF16),
-            pltpu.VMEM((local_count, group_size * text_len, width), F32),
             pltpu.VMEM((128, 128), F32),
             pltpu.VMEM((owners, txt_rows, width), BF16),
-            DMA,
+            DMA((3,)),
             DMA,
             DMA((owners,)),
         ],
@@ -342,15 +350,21 @@
     (partial,) = call(partial_kernel, [shape((dp, 16, 128), BF16)], [VMEM] * 5, 8 * depth * 64)(
         *turned, txt_quarter
     )
-    (mine,) = call(rows_kernel, [shape((owners, 16, 128), F32)], [VMEM], 2 * dp * 2048)(swap(partial, "dp"))
+    everything = swap(partial, "dp")
+    (mine,) = call(rows_kernel, [shape((owners, 16, 128), F32)], [VMEM], 2 * dp * 2048)(everything)
+    feat_img, feat_txt = call(
+        feature_kernel,
+        [shape((img_rows, depth), BF16), shape((txt_rows, depth), BF16)],
+        [VMEM] * 4,
+        2 * (img_rows + txt_rows) * depth * width,
+        grant=FEATURE_GRANT,
+    )(img_back, w_img, txt_back, w_txt)
     final_img, final_txt = call(
         lambda *refs: final_kernel(outer, *refs),
         [shape((16, width), F32), shape((16, width), F32)],
         [VMEM],
         owners * 2048,
     )(swap(mine, NEG))
-    feat_img = jnp.dot(img_back, w_img.T, preferred_element_type=F32).astype(BF16)
-    feat_txt = jnp.dot(txt_back, w_txt.T, preferred_element_type=F32).astype(BF16)
     return (
         feat_img.reshape(img_features.shape),
         feat_txt.reshape(txt_features.shape),

time: 143 us -> 143 us (level)
  Pallas kernels: 16.7 us -> 19.2 us
  matrix products: 2.45 us -> 0 us
    pallas_call x0 -> x1, Pallas kernels: none -> 2.58 us  [window(): call(feature_kernel, [shape((img_rows, depth), BF16), shape((txt_rows, de...]
    dot_general x2 -> x0, matrix products: 2.45 us -> none  [the longest x1 1.44 us: window(): jnp.dot(img_back, w_img.T, preferred_element_type=F32).astype(BF16)]
  transfers between devices with their start and end apart: 7 -> 7, of which waited for: 5 -> 5; matrix products, arithmetic and copies ran while one was open for 2% -> 0% of each run, Pallas kernels for 4% -> 6%
where the time goes in v3:
time: 143 us; the launch traced here: 142 us
  blocking collectives  52.3 us (37%)
  starting transfers between devices  38.2 us (27%)
  waiting for transfers between devices  30.2 us (21%)
  Pallas kernels  19.2 us (13%)
    all_to_all x2, blocking collectives, swap(): return lax.all_to_all(array, axis, 0, 0, tiled=True)  52.3 us
    all_to_all x4, starting transfers between devices, swap(): return lax.all_to_all(array, axis, 0, 0, tiled=True)  29.4 us
    all_to_all x4, waiting for transfers between devices, swap(): return lax.all_to_all(array, axis, 0, 0, tiled=True)  24 us
    ppermute x3, starting transfers between devices, window(): lax.ppermute(turned[turn], 'neg_1', [(k, (k + turn) % 4) for k in range(4)])  8.79 us
    ppermute x3, waiting for transfers between devices, window(): lax.ppermute(turned[turn], 'neg_1', [(k, (k + turn) % 4) for k in range(4)])  6.14 us
    pallas_call x1, Pallas kernels, window(): call(lambda *refs: image_back_kernel(text_len, *refs), [shape((img_rows,...  4.86 us
    pallas_call x1, Pallas kernels, window(): call(lambda *refs: pair_kernel(group_size, img_len, *refs), [shape((owner...  3.33 us
  transfers between devices with their start and end apart: 7, of which 5 were waited for; matrix products, arithmetic and copies ran while one was open for 0% of the time, Pallas kernels for 6%

profile of v3, /device:TPU:6, one launch (start us, length us, event | category | flops | bytes accessed | tf_op | source)
XLA Modules:
  0.0 141.5 jit_solution(6608270837919925485)
XLA Ops:
  0.6 2.4 %shard_map.93 = bf16[12,136,256]{2,1,0:T(8,128)(2,1)} custom-call(s32[2]{0:T(128)} %len_ref.1, bf16[128,1024]{1,0:T(8,128)(2,1)} %bitcast.6, bf16[1024,256]{1,0:T(8,128)(2,1)} %w_txt_ref.1), custom_call_target="tpu_custom_call" | custom-call | flops 67108864 | bytes 1671168 | tf_op jit(solution)/shard_map/pallas_call | solution.py:271
  3.1 13.1 %all-to-all-start = ((bf16[12,136,256]{2,1,0:T(8,128)(2,1)}), bf16[12,136,256]{2,1,0:T(8,128)(2,1)S(1)}, u32[]{:S(2)}, u32[]{:S(2)}) async-start(bf16[12,136,256]{2,1,0:T(8,128)(2,1)} %shard_map.93), calls=%async_computation | async-start | bytes 1671168 | tf_op jit(solution)/shard_map/all_to_all | solution.py:255
  16.2 0.5 shard_map.94.refs_1_.refs_3_
  16.8 10.5 %all-to-all-done.refs_0_.refs_1_ = bf16[12,136,256]{2,1,0:T(8,128)(2,1)S(1)} async-done(((bf16[12,136,256]{2,1,0:T(8,128)(2,1)}), bf16[12,136,256]{2,1,0:T(8,128)(2,1)S(1)}, u32[]{:S(2)}, u32[]{:S(2)}) %all-to-all-start) | async-done | bytes 835616 | tf_op jit(solution)/shard_map/all_to_all | solution.py:255
  27.2 2.4 %shard_map.95 = (bf16[1536,512]{1,0:T(8,128)(2,1)}, f32[12,8,128]{2,1,0:T(8,128)S(1)}) custom-call(bf16[12,136,256]{2,1,0:T(8,128)(2,1)S(1)} %all-to-all-done.refs_0_.refs_1_, bf16[512,256]{1,0:T(8,128)(2,1)S(1)} %shard_map.94.refs_1_.refs_3_), custom_call_target="tpu_custom_call" | custom-call | flops 402653184 | bytes 3244032 | tf_op jit(solution)/shard_map/pallas_call | solution.py:282
  29.7 0.9 copy-done.4
  30.6 9.8 %all_to_all.30.refs_1_ = f32[12,8,128]{2,1,0:T(8,128)S(1)} all-to-all(f32[12,8,128]{2,1,0:T(8,128)S(1)} %get-tuple-element.21.refs_2_), channel_id=1, replica_groups=mesh['dp'=64,'neg_0'=3,'neg_1'=4] {'neg_0','neg_1'}, dimensions={0} | all-to-all | bytes 98304 | tf_op jit(solution)/shard_map/all_to_all | solution.py:255
  40.4 3.3 %shard_map.96 = (bf16[12,128,256]{2,1,0:T(8,128)(2,1)}, f32[32,128,128]{2,1,0:T(8,128)}) custom-call(s32[1,24]{1,0:T(1,128)S(1)} %copy-done.6, f32[12,8,128]{2,1,0:T(8,128)S(1)} %all_to_all.30.refs_1_, f32[12,8,128]{2,1,0:T(8,128)S(1)} %get-tuple-element.21.refs_2_, bf16[512,256]{1,0:T(8,128)(2,1)S(1)} %shard_map.94.refs_1_.refs_3_, ...), custom_call_target="tpu_custom_call" | custom-call | flops 402653184 | bytes 5767168 | tf_op jit(solution)/shard_map/pallas_call | solution.py:298
  43.7 5.4 %all-to-all-start.2 = ((bf16[12,128,256]{2,1,0:T(8,128)(2,1)}), bf16[12,128,256]{2,1,0:T(8,128)(2,1)S(1)}, u32[]{:S(2)}, u32[]{:S(2)}) async-start(bf16[12,128,256]{2,1,0:T(8,128)(2,1)} %get-tuple-element.25), calls=%async_computation.2 | async-start | bytes 1572864 | tf_op jit(solution)/shard_map/all_to_all | solution.py:255
  49.4 10.4 %all-to-all-done.2.all_ref = bf16[12,128,256]{2,1,0:T(8,128)(2,1)S(1)} async-done(((bf16[12,128,256]{2,1,0:T(8,128)(2,1)}), bf16[12,128,256]{2,1,0:T(8,128)(2,1)S(1)}, u32[]{:S(2)}, u32[]{:S(2)}) %all-to-all-start.2) | async-done | bytes 786464 | tf_op jit(solution)/shard_map/all_to_all | solution.py:255
  59.9 1.3 shard_map.99
  61.2 4.5 %all-to-all-start.3 = ((bf16[4,512,128]{2,1,0:T(8,128)(2,1)}), bf16[4,512,128]{2,1,0:T(8,128)(2,1)S(1)}, u32[]{:S(2)}, u32[]{:S(2)}) async-start(bf16[4,512,128]{2,1,0:T(8,128)(2,1)} %get-tuple-element.35), calls=%async_computation.3 | async-start | bytes 1048576 | tf_op jit(solution)/shard_map/all_to_all | solution.py:255
  65.7 4.9 %shard_map.97 = (bf16[512,256]{1,0:T(8,128)(2,1)S(1)}, bf16[512,128]{1,0:T(8,128)(2,1)S(1)}, bf16[512,128]{1,0:T(8,128)(2,1)S(1)}, bf16[512,128]{1,0:T(8,128)(2,1)S(1)}, bf16[512,128]{1,0:T(8,128)(2,1)S(1)}) custom-call(f32[32,128,128]{2,1,0:T(8,128)} %get-tuple-element.23.refs_0_, bf16[12,136,256]{2,1,0:T(8,128)(2,1)} %copy-done.4, ...), custom_call_target="tpu_custom_call" | custom-call | flops 671088640 | bytes 1572864 | tf_op jit(solution)/shard_map/pallas_call | solution.py:315
  70.5 2.1 %collective-permute-start = (bf16[512,128]{1,0:T(8,128)(2,1)S(1)}, bf16[512,128]{1,0:T(8,128)(2,1)S(1)}, u32[]{:S(2)}, u32[]{:S(2)}) collective-permute-start(bf16[512,128]{1,0:T(8,128)(2,1)S(1)} %get-tuple-element.32), channel_id=1, source_target_pairs={{0,1},{1,2},{2,3},{3,0},{4,5},{5,6},{6,7},{7,4},{8,9},{9,10},{10,1... | collective-permute-start | bytes 393224 | tf_op jit(solution)/shard_map/ppermute | solution.py:336
  72.6 4.8 %collective-permute-start.1 = (bf16[512,128]{1,0:T(8,128)(2,1)S(1)}, bf16[512,128]{1,0:T(8,128)(2,1)S(1)}, u32[]{:S(2)}, u32[]{:S(2)}) collective-permute-start(bf16[512,128]{1,0:T(8,128)(2,1)S(1)} %get-tuple-element.33), channel_id=1, source_target_pairs={{0,2},{1,3},{2,0},{3,1},{4,6},{5,7},{6,4},{7,5},{8,10},{9,11},{10,... | collective-permute-start | bytes 393224 | tf_op jit(solution)/shard_map/ppermute | solution.py:336
  77.4 1.9 %collective-permute-start.2 = (bf16[512,128]{1,0:T(8,128)(2,1)S(1)}, bf16[512,128]{1,0:T(8,128)(2,1)S(1)}, u32[]{:S(2)}, u32[]{:S(2)}) collective-permute-start(bf16[512,128]{1,0:T(8,128)(2,1)S(1)} %get-tuple-element.34), channel_id=1, source_target_pairs={{0,3},{1,0},{2,1},{3,2},{4,7},{5,4},{6,5},{7,6},{8,11},{9,8},{10,9... | collective-permute-start | bytes 393224 | tf_op jit(solution)/shard_map/ppermute | solution.py:336
  79.4 1.6 %collective-permute-done.1.refs_2_ = bf16[512,128]{1,0:T(8,128)(2,1)S(1)} collective-permute-done((bf16[512,128]{1,0:T(8,128)(2,1)S(1)}, bf16[512,128]{1,0:T(8,128)(2,1)S(1)}, u32[]{:S(2)}, u32[]{:S(2)}) %collective-permute-start.1) | collective-permute-done | bytes 131104 | tf_op jit(solution)/shard_map/ppermute | solution.py:336
  81.0 4.5 %collective-permute-done.2.refs_3_ = bf16[512,128]{1,0:T(8,128)(2,1)S(1)} collective-permute-done((bf16[512,128]{1,0:T(8,128)(2,1)S(1)}, bf16[512,128]{1,0:T(8,128)(2,1)S(1)}, u32[]{:S(2)}, u32[]{:S(2)}) %collective-permute-start.2) | collective-permute-done | bytes 131104 | tf_op jit(solution)/shard_map/ppermute | solution.py:336
  85.6 42.5 %all_to_all.31.all_ref = bf16[64,16,128]{2,1,0:T(8,128)(2,1)S(1)} all-to-all(bf16[64,16,128]{2,1,0:T(8,128)(2,1)S(1)} %shard_map.101), channel_id=1, replica_groups=mesh['dp'=64,'neg_0'=3,'neg_1'=4] {'dp'}, dimensions={0} | all-to-all | bytes 524288 | tf_op jit(solution)/shard_map/all_to_all | solution.py:255
  128.1 0.7 shard_map.102
  128.8 6.4 %all-to-all-start.5 = ((f32[12,16,128]{2,1,0:T(8,128)}), f32[12,16,128]{2,1,0:T(8,128)S(1)}, u32[]{:S(2)}, u32[]{:S(2)}) async-start(f32[12,16,128]{2,1,0:T(8,128)} %shard_map.102), calls=%async_computation.5 | async-start | bytes 196608 | tf_op jit(solution)/shard_map/all_to_all | solution.py:255
  135.2 2.6 %shard_map.100 = (bf16[512,1024]{1,0:T(8,128)(2,1)}, bf16[128,1024]{1,0:T(8,128)(2,1)}) custom-call(bf16[512,256]{1,0:T(8,128)(2,1)S(1)} %get-tuple-element.24.img_ref, bf16[1024,256]{1,0:T(8,128)(2,1)S(1)} %copy-done.1, bf16[128,256]{1,0:T(8,128)(2,1)S(1)} %get-tuple-element.28.txt_ref, bf16[1024,256]{1,0:T(8,128)(2,1)} %w_txt_ref.1), custom_call_target="tpu_custom_call" | custom-call | flops 335544320 | bytes 2621440 | tf_op jit(solution)/shard_map/pallas_call | solution.py:355
  137.8 3.1 %all-to-all-done.5.refs_0_ = f32[12,16,128]{2,1,0:T(8,128)S(1)} async-done(((f32[12,16,128]{2,1,0:T(8,128)}), f32[12,16,128]{2,1,0:T(8,128)S(1)}, u32[]{:S(2)}, u32[]{:S(2)}) %all-to-all-start.5) | async-done | bytes 98336 | tf_op jit(solution)/shard_map/all_to_all | solution.py:255
  140.9 0.6 shard_map.103
  (17 shorter events, 0.5 us)
Async XLA Ops:
  0.6 15.6 %copy-start = (bf16[1024,256]{1,0:T(8,128)(2,1)S(1)}, bf16[1024,256]{1,0:T(8,128)(2,1)}, u32[]{:S(2)}) copy-start(bf16[1024,256]{1,0:T(8,128)(2,1)} %w_img_ref.1) | copy-start | bytes 1572868
  3.1 13.2 %copy-start.3 = (bf16[2,256,1024]{2,1,0:T(8,128)(2,1)S(1)}, bf16[2,256,1024]{2,1,0:T(8,128)(2,1)}, u32[]{:S(2)}) copy-start(bf16[2,256,1024]{2,1,0:T(8,128)(2,1)} %param.6) | copy-start | bytes 3145732
  3.1 24.2 %all-to-all-start = ((bf16[12,136,256]{2,1,0:T(8,128)(2,1)}), bf16[12,136,256]{2,1,0:T(8,128)(2,1)S(1)}, u32[]{:S(2)}, u32[]{:S(2)}) async-start(bf16[12,136,256]{2,1,0:T(8,128)(2,1)} %shard_map.93), calls=%async_computation | async-start | bytes 1671168 | tf_op jit(solution)/shard_map/all_to_all | solution.py:255
  16.2 24.1 %copy-start.6 = (s32[1,24]{1,0:T(1,128)S(1)}, s32[1,24]{1,0:T(1,128)}, u32[]{:S(2)}) copy-start(s32[1,24]{1,0:T(1,128)} %refs_0_.1) | copy-start | bytes 292
  29.7 0.9 copy-start.4
  30.6 18.5 %copy-start.2 = (bf16[1024,256]{1,0:T(8,128)(2,1)S(1)}, bf16[1024,256]{1,0:T(8,128)(2,1)}, u32[]{:S(2)}) copy-start(bf16[1024,256]{1,0:T(8,128)(2,1)} %w_txt_ref.1) | copy-start | bytes 1572868
  30.6 18.5 %copy-start.5 = (bf16[2,64,1024]{2,1,0:T(8,128)(2,1)S(1)}, bf16[2,64,1024]{2,1,0:T(8,128)(2,1)}, u32[]{:S(2)}) copy-start(bf16[2,64,1024]{2,1,0:T(8,128)(2,1)} %param.7) | copy-start | bytes 786436
  43.7 16.2 %all-to-all-start.2 = ((bf16[12,128,256]{2,1,0:T(8,128)(2,1)}), bf16[12,128,256]{2,1,0:T(8,128)(2,1)S(1)}, u32[]{:S(2)}, u32[]{:S(2)}) async-start(bf16[12,128,256]{2,1,0:T(8,128)(2,1)} %get-tuple-element.25), calls=%async_computation.2 | async-start | bytes 1572864 | tf_op jit(solution)/shard_map/all_to_all | solution.py:255
  61.2 24.3 %all-to-all-start.3 = ((bf16[4,512,128]{2,1,0:T(8,128)(2,1)}), bf16[4,512,128]{2,1,0:T(8,128)(2,1)S(1)}, u32[]{:S(2)}, u32[]{:S(2)}) async-start(bf16[4,512,128]{2,1,0:T(8,128)(2,1)} %get-tuple-element.35), calls=%async_computation.3 | async-start | bytes 1048576 | tf_op jit(solution)/shard_map/all_to_all | solution.py:255
  70.5 64.7 %copy-start.1 = (bf16[1024,256]{1,0:T(8,128)(2,1)S(1)}, bf16[1024,256]{1,0:T(8,128)(2,1)}, u32[]{:S(2)}) copy-start(bf16[1024,256]{1,0:T(8,128)(2,1)} %w_img_ref.1) | copy-start | bytes 1572868
  70.5 8.8 %collective-permute-start = (bf16[512,128]{1,0:T(8,128)(2,1)S(1)}, bf16[512,128]{1,0:T(8,128)(2,1)S(1)}, u32[]{:S(2)}, u32[]{:S(2)}) collective-permute-start(bf16[512,128]{1,0:T(8,128)(2,1)S(1)} %get-tuple-element.32), channel_id=1, source_target_pairs={{0,1},{1,2},{2,3},{3,0},{4,5},{5,6},{6,7},{7,4},{8,9},{9,10},{10,1... | collective-permute-start | bytes 393224 | tf_op jit(solution)/shard_map/ppermute | solution.py:336
  72.6 8.4 %collective-permute-start.1 = (bf16[512,128]{1,0:T(8,128)(2,1)S(1)}, bf16[512,128]{1,0:T(8,128)(2,1)S(1)}, u32[]{:S(2)}, u32[]{:S(2)}) collective-permute-start(bf16[512,128]{1,0:T(8,128)(2,1)S(1)} %get-tuple-element.33), channel_id=1, source_target_pairs={{0,2},{1,3},{2,0},{3,1},{4,6},{5,7},{6,4},{7,5},{8,10},{9,11},{10,... | collective-permute-start | bytes 393224 | tf_op jit(solution)/shard_map/ppermute | solution.py:336
  77.4 8.1 %collective-permute-start.2 = (bf16[512,128]{1,0:T(8,128)(2,1)S(1)}, bf16[512,128]{1,0:T(8,128)(2,1)S(1)}, u32[]{:S(2)}, u32[]{:S(2)}) collective-permute-start(bf16[512,128]{1,0:T(8,128)(2,1)S(1)} %get-tuple-element.34), channel_id=1, source_target_pairs={{0,3},{1,0},{2,1},{3,2},{4,7},{5,4},{6,5},{7,6},{8,11},{9,8},{10,9... | collective-permute-start | bytes 393224 | tf_op jit(solution)/shard_map/ppermute | solution.py:336
  128.8 12.1 %all-to-all-start.5 = ((f32[12,16,128]{2,1,0:T(8,128)}), f32[12,16,128]{2,1,0:T(8,128)S(1)}, u32[]{:S(2)}, u32[]{:S(2)}) async-start(f32[12,16,128]{2,1,0:T(8,128)} %shard_map.102), calls=%async_computation.5 | async-start | bytes 196608 | tf_op jit(solution)/shard_map/all_to_all | solution.py:255

commit v4 on v3

--- a/solution.py
+++ b/solution.py
@@ -167,7 +167,7 @@
 def image_back_kernel(
     text_len, pair_hbm, g_hbm, wt_hbm, w_hbm, x_hbm, back_hbm, *refs
 ):
-    turned, refs = refs[:4], refs[4:]
+    kept, given, refs = refs[0], refs[1], refs[2:]
     pair_ref, g_ref, wt_ref, w_ref, x_ref, scaled_ref, back_ref, pay_ref, in_sem, out_sem = refs
     owners = g_ref.shape[0]
     pair = copy(pair_hbm.at[0], pair_ref, in_sem.at[4])
@@ -196,11 +196,9 @@
     for j in range(4):
         h, k = j // 2, j % 2
         piece = tiles[:, 8 * h : 8 * h + 8, 128 * k : 128 * k + 128]
-        pay_ref[j] = piece.reshape(pay_ref.shape[1:]).astype(BF16)
-    me = lax.axis_index("neg_1")
-    moving = [
-        copy(pay_ref.at[lax.rem(me + turn, 4)], target, out_sem.at[turn]) for turn, target in enumerate(turned)
-    ]
+        pay_ref[k, h] = piece.reshape(-1, 128).astype(BF16)
+    mine = lax.rem(lax.axis_index("dp"), 2)
+    moving = [copy(pay_ref.at[mine], kept, out_sem.at[0]), copy(pay_ref.at[1 - mine], given, out_sem.at[1])]
     for one in moving:
         one.wait()
     result.wait()
@@ -219,6 +217,12 @@
         pay_ref[j] = piece.reshape(pay_ref.shape[1:]).astype(BF16)
 
 
+def half_kernel(kept_ref, given_ref, mine_ref, next_ref):
+    side = lax.rem(lax.axis_index("dp") // 2, 2)
+    mine_ref[...] = (kept_ref[side].astype(F32) + given_ref[side].astype(F32)).astype(BF16)
+    next_ref[...] = (kept_ref[1 - side].astype(F32) + given_ref[1 - side].astype(F32)).astype(BF16)
+
+
 def feature_kernel(img_ref, w_img_ref, txt_ref, w_txt_ref, img_out, txt_out):
     img_out[...] = along_last(img_ref[...], w_img_ref[...]).astype(BF16)
     txt_out[...] = along_last(txt_ref[...], w_txt_ref[...]).astype(BF16)
@@ -235,20 +239,23 @@
 
 
 def rows_kernel(all_ref, out_ref):
-    total = jnp.sum(all_ref[...].astype(F32), axis=0)
+    img = jnp.sum(all_ref[:, :8, :].astype(F32).reshape(-1, 4, 8, 128), axis=0).reshape(32, 128)
+    txt = jnp.sum(all_ref[:, 8:, :].astype(F32), axis=0)
     for d in range(out_ref.shape[0]):
-        out_ref[d] = total
+        out_ref[d, :32, :] = img.astype(BF16)
+        out_ref[d, 32:, :] = txt.astype(BF16)
 
 
 def final_kernel(outer, all_ref, img_ref, txt_ref):
     inner = all_ref.shape[0] // outer
+    img = jnp.sum(all_ref[:, :32, :].astype(F32), axis=0)
     for j in range(inner):
-        total = all_ref[j]
+        txt = all_ref[j, 32:].astype(F32)
         for i in range(1, outer):
-            total += all_ref[i * inner + j]
+            txt += all_ref[i * inner + j, 32:].astype(F32)
         h, k = j // 2, j % 2
-        img_ref[8 * h : 8 * h + 8, 128 * k : 128 * k + 128] = total[:8]
-        txt_ref[8 * h : 8 * h + 8, 128 * k : 128 * k + 128] = total[8:]
+        img_ref[8 * h : 8 * h + 8, 128 * k : 128 * k + 128] = img[8 * j : 8 * j + 8]
+        txt_ref[8 * h : 8 * h + 8, 128 * k : 128 * k + 128] = txt
 
 
 def swap(array, axis):
@@ -312,9 +319,9 @@
         grant=PAIR_GRANT,
     )(pairs, everyone, own, img_half, weights)
     arrived = swap(text_terms, NEG)
-    img_back, *turned = call(
+    img_back, kept, given = call(
         lambda *refs: image_back_kernel(text_len, *refs),
-        [shape((img_rows, width), BF16)] + [shape((depth // 2, 128), BF16)] * 4,
+        [shape((img_rows, width), BF16)] + [shape((2, depth // 2, 128), BF16)] * 2,
         [HBM, HBM, HBM, HBM, HBM],
         2 * img_rows * width * (group_size * text_len + depth),
         [
@@ -325,15 +332,18 @@
             pltpu.VMEM((img_rows, depth), BF16),
             pltpu.VMEM((2, group_size * text_len, width), BF16),
             pltpu.VMEM((img_rows, width), BF16),
-            pltpu.VMEM((4, depth // 2, 128), BF16),
+            pltpu.VMEM((2, 2, depth // 2, 128), BF16),
             DMA((5,)),
             DMA((5,)),
         ],
-        places=[HBM] * 5,
+        places=[HBM] * 3,
         grant=BACK_GRANT,
     )(pair, group, weights, w_img, img_flat)
-    for turn in range(1, 4):
-        turned[turn] = lax.ppermute(turned[turn], "neg_1", [(k, (k + turn) % 4) for k in range(4)])
+    given = lax.ppermute(given, "dp", [(d, d ^ 1) for d in range(dp)])
+    img_mine, img_given = call(
+        half_kernel, [shape((depth // 2, 128), BF16)] * 2, [VMEM, VMEM], 2 * depth * 128
+    )(kept, given)
+    img_given = lax.ppermute(img_given, "dp", [(d, d ^ 2) for d in range(dp)])
     txt_unit, txt_inv = call(
         unit_kernel,
         [shape((txt_rows, width), F32), shape((txt_rows, 128), F32)],
@@ -347,11 +357,11 @@
         2 * txt_rows * width * depth,
     )(arrived, txt_unit, txt_inv, txt_flat)
     txt_quarter = swap(txt_pieces, "neg_1")
-    (partial,) = call(partial_kernel, [shape((dp, 16, 128), BF16)], [VMEM] * 5, 8 * depth * 64)(
-        *turned, txt_quarter
+    (partial,) = call(partial_kernel, [shape((dp, 16, 128), BF16)], [VMEM] * 3, 8 * depth * 64)(
+        img_mine, img_given, txt_quarter
     )
     everything = swap(partial, "dp")
-    (mine,) = call(rows_kernel, [shape((owners, 16, 128), F32)], [VMEM], 2 * dp * 2048)(everything)
+    (mine,) = call(rows_kernel, [shape((owners, 40, 128), BF16)], [VMEM], 2 * dp * 2048)(everything)
     feat_img, feat_txt = call(
         feature_kernel,
         [shape((img_rows, depth), BF16), shape((txt_rows, depth), BF16)],

time: 143 us -> 131 us (0.916)
  waiting for transfers between devices: 30.2 us -> 20.9 us
  blocking collectives: 52.3 us -> 49.6 us
    all_to_all x4, waiting for transfers between devices: 24 us -> 17.9 us  [swap(): return lax.all_to_all(array, axis, 0, 0, tiled=True)]
    ppermute x3 -> x2, waiting for transfers between devices: 6.14 us -> 2.93 us  [the longest x1 2.93 us: window(): img_given = lax.ppermute(img_given, 'dp', [(d, d ^ 2) for d in range(dp)])]
    all_to_all x2, blocking collectives: 52.3 us -> 49.6 us  [swap(): return lax.all_to_all(array, axis, 0, 0, tiled=True)]
    ppermute x3 -> x2, starting transfers between devices: 8.79 us -> 8.61 us  [the longest x1 6.69 us: window(): img_given = lax.ppermute(img_given, 'dp', [(d, d ^ 2) for d in range(dp)])]
  transfers between devices with their start and end apart: 7 -> 6, of which waited for: 5 -> 4; matrix products, arithmetic and copies ran while one was open for 0% -> 0% of each run, Pallas kernels for 6% -> 7%
where the time goes in v4:
time: 131 us; the launch traced here: 129 us
  blocking collectives  49.6 us (38%)
  starting transfers between devices  38.5 us (29%)
  waiting for transfers between devices  20.9 us (16%)
  Pallas kernels  18.7 us (14%)
    all_to_all x2, blocking collectives, swap(): return lax.all_to_all(array, axis, 0, 0, tiled=True)  49.6 us
    all_to_all x4, starting transfers between devices, swap(): return lax.all_to_all(array, axis, 0, 0, tiled=True)  29.9 us
    all_to_all x4, waiting for transfers between devices, swap(): return lax.all_to_all(array, axis, 0, 0, tiled=True)  17.9 us
    ppermute x1, starting transfers between devices, window(): img_given = lax.ppermute(img_given, 'dp', [(d, d ^ 2) for d in range(dp)])  6.69 us
    pallas_call x1, Pallas kernels, window(): call(lambda *refs: image_back_kernel(text_len, *refs), [shape((img_rows,...  4.22 us
    pallas_call x1, Pallas kernels, window(): call(lambda *refs: pair_kernel(group_size, img_len, *refs), [shape((owner...  3.34 us
    ppermute x1, waiting for transfers between devices, window(): img_given = lax.ppermute(img_given, 'dp', [(d, d ^ 2) for d in range(dp)])  2.93 us
  transfers between devices with their start and end apart: 6, of which 4 were waited for; matrix products, arithmetic and copies ran while one was open for 0% of the time, Pallas kernels for 7%

profile of v4, /device:TPU:6, one launch (start us, length us, event | category | flops | bytes accessed | tf_op | source)
XLA Modules:
  0.0 129.2 jit_solution(15722539571624281471)
XLA Ops:
  0.6 2.4 %shard_map.93 = bf16[12,136,256]{2,1,0:T(8,128)(2,1)} custom-call(s32[2]{0:T(128)} %len_ref.1, bf16[128,1024]{1,0:T(8,128)(2,1)} %bitcast.6, bf16[1024,256]{1,0:T(8,128)(2,1)} %w_txt_ref.1), custom_call_target="tpu_custom_call" | custom-call | flops 67108864 | bytes 1671168 | tf_op jit(solution)/shard_map/pallas_call | solution.py:278
  3.1 13.1 %all-to-all-start = ((bf16[12,136,256]{2,1,0:T(8,128)(2,1)}), bf16[12,136,256]{2,1,0:T(8,128)(2,1)S(1)}, u32[]{:S(2)}, u32[]{:S(2)}) async-start(bf16[12,136,256]{2,1,0:T(8,128)(2,1)} %shard_map.93), calls=%async_computation | async-start | bytes 1671168 | tf_op jit(solution)/shard_map/all_to_all | solution.py:262
  16.2 0.5 shard_map.94.refs_1_.refs_3_
  16.8 10.5 %all-to-all-done.refs_0_.refs_1_ = bf16[12,136,256]{2,1,0:T(8,128)(2,1)S(1)} async-done(((bf16[12,136,256]{2,1,0:T(8,128)(2,1)}), bf16[12,136,256]{2,1,0:T(8,128)(2,1)S(1)}, u32[]{:S(2)}, u32[]{:S(2)}) %all-to-all-start) | async-done | bytes 835616 | tf_op jit(solution)/shard_map/all_to_all | solution.py:262
  27.2 2.4 %shard_map.95 = (bf16[1536,512]{1,0:T(8,128)(2,1)}, f32[12,8,128]{2,1,0:T(8,128)S(1)}) custom-call(bf16[12,136,256]{2,1,0:T(8,128)(2,1)S(1)} %all-to-all-done.refs_0_.refs_1_, bf16[512,256]{1,0:T(8,128)(2,1)S(1)} %shard_map.94.refs_1_.refs_3_), custom_call_target="tpu_custom_call" | custom-call | flops 402653184 | bytes 3244032 | tf_op jit(solution)/shard_map/pallas_call | solution.py:289
  29.7 0.9 copy-done.4
  30.6 9.8 %all_to_all.30.refs_1_ = f32[12,8,128]{2,1,0:T(8,128)S(1)} all-to-all(f32[12,8,128]{2,1,0:T(8,128)S(1)} %get-tuple-element.21.refs_2_), channel_id=1, replica_groups=mesh['dp'=64,'neg_0'=3,'neg_1'=4] {'neg_0','neg_1'}, dimensions={0} | all-to-all | bytes 98304 | tf_op jit(solution)/shard_map/all_to_all | solution.py:262
  40.4 3.3 %shard_map.96 = (bf16[12,128,256]{2,1,0:T(8,128)(2,1)}, f32[32,128,128]{2,1,0:T(8,128)}) custom-call(s32[1,24]{1,0:T(1,128)S(1)} %copy-done.6, f32[12,8,128]{2,1,0:T(8,128)S(1)} %all_to_all.30.refs_1_, f32[12,8,128]{2,1,0:T(8,128)S(1)} %get-tuple-element.21.refs_2_, bf16[512,256]{1,0:T(8,128)(2,1)S(1)} %shard_map.94.refs_1_.refs_3_, ...), custom_call_target="tpu_custom_call" | custom-call | flops 402653184 | bytes 5767168 | tf_op jit(solution)/shard_map/pallas_call | solution.py:305
  43.7 5.4 %all-to-all-start.2 = ((bf16[12,128,256]{2,1,0:T(8,128)(2,1)}), bf16[12,128,256]{2,1,0:T(8,128)(2,1)S(1)}, u32[]{:S(2)}, u32[]{:S(2)}) async-start(bf16[12,128,256]{2,1,0:T(8,128)(2,1)} %get-tuple-element.25), calls=%async_computation.2 | async-start | bytes 1572864 | tf_op jit(solution)/shard_map/all_to_all | solution.py:262
  49.1 0.3 shard_map.98
  49.5 4.2 %shard_map.97 = (bf16[512,256]{1,0:T(8,128)(2,1)S(1)}, bf16[2,512,128]{2,1,0:T(8,128)(2,1)S(1)}, bf16[2,512,128]{2,1,0:T(8,128)(2,1)S(1)}) custom-call(f32[32,128,128]{2,1,0:T(8,128)} %get-tuple-element.23.refs_0_, bf16[12,136,256]{2,1,0:T(8,128)(2,1)} %copy-done.4, bf16[1536,512]{1,0:T(8,128)(2,1)} %get-tuple-element.22.refs_4_.refs_2_, ...), custom_call_target="tpu_custom_call" | custom-call | flops 671088640 | bytes 1572864 | tf_op jit(solution)/shard_map/pallas_call | solution.py:322
  53.7 1.9 %collective-permute-start = (bf16[2,512,128]{2,1,0:T(8,128)(2,1)S(1)}, bf16[2,512,128]{2,1,0:T(8,128)(2,1)S(1)}, u32[]{:S(2)}, u32[]{:S(2)}) collective-permute-start(bf16[2,512,128]{2,1,0:T(8,128)(2,1)S(1)} %get-tuple-element.32), channel_id=1, source_target_pairs={{0,12},{12,0},{24,36},{36,24},{48,60},{60,48},{72,84},{84,72},{96,... | collective-permute-start | bytes 786440 | tf_op jit(solution)/shard_map/ppermute | solution.py:342
  55.6 4.2 %all-to-all-done.2.all_ref = bf16[12,128,256]{2,1,0:T(8,128)(2,1)S(1)} async-done(((bf16[12,128,256]{2,1,0:T(8,128)(2,1)}), bf16[12,128,256]{2,1,0:T(8,128)(2,1)S(1)}, u32[]{:S(2)}, u32[]{:S(2)}) %all-to-all-start.2) | async-done | bytes 786464 | tf_op jit(solution)/shard_map/all_to_all | solution.py:262
  59.8 1.3 shard_map.99
  61.1 4.6 %all-to-all-start.3 = ((bf16[4,512,128]{2,1,0:T(8,128)(2,1)}), bf16[4,512,128]{2,1,0:T(8,128)(2,1)S(1)}, u32[]{:S(2)}, u32[]{:S(2)}) async-start(bf16[4,512,128]{2,1,0:T(8,128)(2,1)} %get-tuple-element.35), calls=%async_computation.3 | async-start | bytes 1048576 | tf_op jit(solution)/shard_map/all_to_all | solution.py:262
  65.8 6.7 %collective-permute-start.1 = (bf16[512,128]{1,0:T(8,128)(2,1)S(1)}, bf16[512,128]{1,0:T(8,128)(2,1)S(1)}, u32[]{:S(2)}, u32[]{:S(2)}) collective-permute-start(bf16[512,128]{1,0:T(8,128)(2,1)S(1)} %get-tuple-element.34), channel_id=1, source_target_pairs={{0,24},{12,36},{24,0},{36,12},{48,72},{60,84},{72,48},{84,60},{96,... | collective-permute-start | bytes 393224 | tf_op jit(solution)/shard_map/ppermute | solution.py:346
  72.5 2.9 %collective-permute-done.1.refs_1_ = bf16[512,128]{1,0:T(8,128)(2,1)S(1)} collective-permute-done((bf16[512,128]{1,0:T(8,128)(2,1)S(1)}, bf16[512,128]{1,0:T(8,128)(2,1)S(1)}, u32[]{:S(2)}, u32[]{:S(2)}) %collective-permute-start.1) | collective-permute-done | bytes 131104 | tf_op jit(solution)/shard_map/ppermute | solution.py:346
  75.4 0.1 shard_map.102
  75.5 39.8 %all_to_all.31.all_ref = bf16[64,16,128]{2,1,0:T(8,128)(2,1)S(1)} all-to-all(bf16[64,16,128]{2,1,0:T(8,128)(2,1)S(1)} %shard_map.102), channel_id=1, replica_groups=mesh['dp'=64,'neg_0'=3,'neg_1'=4] {'dp'}, dimensions={0} | all-to-all | bytes 524288 | tf_op jit(solution)/shard_map/all_to_all | solution.py:262
  115.3 0.7 shard_map.103
  116.1 6.7 %all-to-all-start.5 = ((bf16[12,40,128]{2,1,0:T(8,128)(2,1)}), bf16[12,40,128]{2,1,0:T(8,128)(2,1)S(1)}, u32[]{:S(2)}, u32[]{:S(2)}) async-start(bf16[12,40,128]{2,1,0:T(8,128)(2,1)} %shard_map.103), calls=%async_computation.5 | async-start | bytes 245760 | tf_op jit(solution)/shard_map/all_to_all | solution.py:262
  122.7 2.6 %shard_map.100 = (bf16[512,1024]{1,0:T(8,128)(2,1)}, bf16[128,1024]{1,0:T(8,128)(2,1)}) custom-call(bf16[512,256]{1,0:T(8,128)(2,1)S(1)} %get-tuple-element.24.img_ref, bf16[1024,256]{1,0:T(8,128)(2,1)S(1)} %copy-done.1, bf16[128,256]{1,0:T(8,128)(2,1)S(1)} %get-tuple-element.28.txt_ref, bf16[1024,256]{1,0:T(8,128)(2,1)} %w_txt_ref.1), custom_call_target="tpu_custom_call" | custom-call | flops 335544320 | bytes 2621440 | tf_op jit(solution)/shard_map/pallas_call | solution.py:365
  125.3 3.3 %all-to-all-done.5.refs_0_ = bf16[12,40,128]{2,1,0:T(8,128)(2,1)S(1)} async-done(((bf16[12,40,128]{2,1,0:T(8,128)(2,1)}), bf16[12,40,128]{2,1,0:T(8,128)(2,1)S(1)}, u32[]{:S(2)}, u32[]{:S(2)}) %all-to-all-start.5) | async-done | bytes 122912 | tf_op jit(solution)/shard_map/all_to_all | solution.py:262
  128.6 0.6 shard_map.104
  (16 shorter events, 0.1 us)
Async XLA Ops:
  0.6 15.6 %copy-start = (bf16[1024,256]{1,0:T(8,128)(2,1)S(1)}, bf16[1024,256]{1,0:T(8,128)(2,1)}, u32[]{:S(2)}) copy-start(bf16[1024,256]{1,0:T(8,128)(2,1)} %w_img_ref.1) | copy-start | bytes 1572868
  3.1 13.2 %copy-start.3 = (bf16[2,256,1024]{2,1,0:T(8,128)(2,1)S(1)}, bf16[2,256,1024]{2,1,0:T(8,128)(2,1)}, u32[]{:S(2)}) copy-start(bf16[2,256,1024]{2,1,0:T(8,128)(2,1)} %param.6) | copy-start | bytes 3145732
  3.1 24.2 %all-to-all-start = ((bf16[12,136,256]{2,1,0:T(8,128)(2,1)}), bf16[12,136,256]{2,1,0:T(8,128)(2,1)S(1)}, u32[]{:S(2)}, u32[]{:S(2)}) async-start(bf16[12,136,256]{2,1,0:T(8,128)(2,1)} %shard_map.93), calls=%async_computation | async-start | bytes 1671168 | tf_op jit(solution)/shard_map/all_to_all | solution.py:262
  16.2 24.2 %copy-start.6 = (s32[1,24]{1,0:T(1,128)S(1)}, s32[1,24]{1,0:T(1,128)}, u32[]{:S(2)}) copy-start(s32[1,24]{1,0:T(1,128)} %refs_0_.1) | copy-start | bytes 292
  29.7 0.9 copy-start.4
  30.6 18.6 %copy-start.2 = (bf16[1024,256]{1,0:T(8,128)(2,1)S(1)}, bf16[1024,256]{1,0:T(8,128)(2,1)}, u32[]{:S(2)}) copy-start(bf16[1024,256]{1,0:T(8,128)(2,1)} %w_txt_ref.1) | copy-start | bytes 1572868
  30.6 18.6 %copy-start.5 = (bf16[2,64,1024]{2,1,0:T(8,128)(2,1)S(1)}, bf16[2,64,1024]{2,1,0:T(8,128)(2,1)}, u32[]{:S(2)}) copy-start(bf16[2,64,1024]{2,1,0:T(8,128)(2,1)} %param.7) | copy-start | bytes 786436
  43.7 16.1 %all-to-all-start.2 = ((bf16[12,128,256]{2,1,0:T(8,128)(2,1)}), bf16[12,128,256]{2,1,0:T(8,128)(2,1)S(1)}, u32[]{:S(2)}, u32[]{:S(2)}) async-start(bf16[12,128,256]{2,1,0:T(8,128)(2,1)} %get-tuple-element.25), calls=%async_computation.2 | async-start | bytes 1572864 | tf_op jit(solution)/shard_map/all_to_all | solution.py:262
  53.7 12.0 %collective-permute-start = (bf16[2,512,128]{2,1,0:T(8,128)(2,1)S(1)}, bf16[2,512,128]{2,1,0:T(8,128)(2,1)S(1)}, u32[]{:S(2)}, u32[]{:S(2)}) collective-permute-start(bf16[2,512,128]{2,1,0:T(8,128)(2,1)S(1)} %get-tuple-element.32), channel_id=1, source_target_pairs={{0,12},{12,0},{24,36},{36,24},{48,60},{60,48},{72,84},{84,72},{96,... | collective-permute-start | bytes 786440 | tf_op jit(solution)/shard_map/ppermute | solution.py:342
  61.1 61.6 %copy-start.1 = (bf16[1024,256]{1,0:T(8,128)(2,1)S(1)}, bf16[1024,256]{1,0:T(8,128)(2,1)}, u32[]{:S(2)}) copy-start(bf16[1024,256]{1,0:T(8,128)(2,1)} %w_img_ref.1) | copy-start | bytes 1572868
  61.1 14.3 %all-to-all-start.3 = ((bf16[4,512,128]{2,1,0:T(8,128)(2,1)}), bf16[4,512,128]{2,1,0:T(8,128)(2,1)S(1)}, u32[]{:S(2)}, u32[]{:S(2)}) async-start(bf16[4,512,128]{2,1,0:T(8,128)(2,1)} %get-tuple-element.35), calls=%async_computation.3 | async-start | bytes 1048576 | tf_op jit(solution)/shard_map/all_to_all | solution.py:262
  65.8 9.6 %collective-permute-start.1 = (bf16[512,128]{1,0:T(8,128)(2,1)S(1)}, bf16[512,128]{1,0:T(8,128)(2,1)S(1)}, u32[]{:S(2)}, u32[]{:S(2)}) collective-permute-start(bf16[512,128]{1,0:T(8,128)(2,1)S(1)} %get-tuple-element.34), channel_id=1, source_target_pairs={{0,24},{12,36},{24,0},{36,12},{48,72},{60,84},{72,48},{84,60},{96,... | collective-permute-start | bytes 393224 | tf_op jit(solution)/shard_map/ppermute | solution.py:346
  116.1 12.6 %all-to-all-start.5 = ((bf16[12,40,128]{2,1,0:T(8,128)(2,1)}), bf16[12,40,128]{2,1,0:T(8,128)(2,1)S(1)}, u32[]{:S(2)}, u32[]{:S(2)}) async-start(bf16[12,40,128]{2,1,0:T(8,128)(2,1)} %shard_map.103), calls=%async_computation.5 | async-start | bytes 245760 | tf_op jit(solution)/shard_map/all_to_all | solution.py:262
